TPU v7x, 32 devices: a whole 2x2x4 slice. The times are simulated.
32 devices in a mesh: dp: 16 (over z, y, core), seq: 2 (over x).
Axes of the slice: x: 2, y: 2, z: 4, core: 2. Of those that a mesh axis runs over, the one named last changes fastest.
Arguments:
- inputs: bfloat16 [2, 16, 768, 256], P(None, 'dp', 'seq'), may hold values from -6 to 6
- lengths: int32 [2, 16], P(None, 'dp'), may hold values from 1 to 768, 9216 in all within a row
- cotangent: bfloat16 [2, 16, 768, 256], P(None, 'dp', 'seq'), may hold values from -6 to 6
- feed_in: bfloat16 [2, 256, 1024], P(None, None, ('dp', 'seq')), may hold values from -0.375 to 0.375
- feed_in_bias: bfloat16 [2, 1024], P(None, ('dp', 'seq')), may hold values from -3 to 3
- feed_out: bfloat16 [2, 1024, 256], P(None, ('dp', 'seq')), may hold values from -0.375 to 0.375
- attend_in: bfloat16 [4, 256, 256], P(None, None, ('dp', 'seq')), may hold values from -0.375 to 0.375
- attend_out: bfloat16 [256, 256], P(None, ('dp', 'seq')), may hold values from -1.5 to 1.5
- point_in: bfloat16 [256, 512], P(None, ('dp', 'seq')), may hold values from -0.375 to 0.375
- point_in_bias: bfloat16 [512], P(('dp', 'seq')), may hold values from -3 to 3
- depth_kernel: bfloat16 [31, 256], P(None, ('dp', 'seq')), may hold values from -1 to 1
- point_out: bfloat16 [256, 256], P(None, ('dp', 'seq')), may hold values from -0.5 to 0.5
- gains: bfloat16 [6, 256], P(None, ('dp', 'seq')), may hold values from 0.25 to 1.75
- biases: bfloat16 [14, 256], P(None, ('dp', 'seq')), may hold values from -3 to 3
Outputs:
- layer_out: bfloat16 [2, 16, 768, 256], P(None, 'dp', 'seq')
- input_grad: float32 [2, 16, 768, 256], P(None, 'dp', 'seq')
- feed_in_grad: float32 [2, 256, 1024], P(None, None, ('dp', 'seq'))
- feed_in_bias_grad: float32 [2, 1024], P(None, ('dp', 'seq'))
- feed_out_grad: float32 [2, 1024, 256], P(None, ('dp', 'seq'))
- attend_in_grad: float32 [4, 256, 256], P(None, None, ('dp', 'seq'))
- attend_out_grad: float32 [256, 256], P(None, ('dp', 'seq'))
- point_in_grad: float32 [256, 512], P(None, ('dp', 'seq'))
- point_in_bias_grad: float32 [512], P(('dp', 'seq'))
- depth_kernel_grad: float32 [31, 256], P(None, ('dp', 'seq'))
- point_out_grad: float32 [256, 256], P(None, ('dp', 'seq'))
- gains_grad: float32 [6, 256], P(None, ('dp', 'seq'))
- biases_grad: float32 [14, 256], P(None, ('dp', 'seq'))
Inputs may be any that keep to these rules, and one draw needn't show every extreme that they name: Within each micro-batch the longest sequence has 768 tokens and the lengths sum to 9216.
All inputs are finite; a program needn't handle non-finite values. No bound on the sum of `lengths` on one device may be relied on, other than what follows from the above.
Results may differ from a plain program's by a relative error of at most 0.025.
Values may be sent and summed in bfloat16 or wider, within the bound.
No kernel may reach another device: no remote copies, remote signals or barrier semaphores. Data moves between devices by JAX's collectives and lax.ppermute only.
A program may use at most 192 MiB of HBM per device.

v0:
```python
import math

import jax
import jax.numpy as jnp
from jax import lax
from jax.sharding import PartitionSpec as P

HEAD = 64


EPSILON = 1e-05
HIGHEST = lax.Precision.HIGHEST
MASKED = -1000000000.0


def with_halo(cells, sides, width):
    for axis, dim in sides:
        count = lax.axis_size(axis)
        ends = count - 1
        head = lax.slice_in_dim(cells, 0, width, axis=dim)
        tail = lax.slice_in_dim(cells, cells.shape[dim] - width, cells.shape[dim], axis=dim)
        cells = jnp.concatenate(
            [
                lax.ppermute(tail, axis, [(i, (i + 1) % count) for i in range(ends)]),
                cells,
                lax.ppermute(head, axis, [((i + 1) % count, i) for i in range(ends)]),
            ],
            axis=dim,
        )
    return cells


def layer_norm(value, gain, shift):
    center = jnp.mean(value, -1, keepdims=True)
    spread = value - center
    variance = jnp.mean(spread * spread, -1, keepdims=True)
    return spread * lax.rsqrt(variance + EPSILON) * gain + shift


def norm_backward(gradient, value, gain, shift):
    pull = jax.vjp(layer_norm, value, gain, shift)[1]
    return pull(gradient)


def sinusoid(offsets, width):
    frequency = jnp.exp(
        jnp.arange(width // 2, dtype=jnp.float32) * (-2.0 * math.log(10000.0) / width)
    )
    angles = offsets.astype(jnp.float32)[:, None] * frequency[None, :]
    return jnp.concatenate([jnp.sin(angles), jnp.cos(angles)], axis=1)


def relative_shift(scores, count):
    row_count = scores.shape[-2]
    span = scores.shape[-1]
    leading = scores.shape[:-2]
    flipped = jnp.flip(scores, -1).reshape(leading + (row_count * span,))
    picked = lax.slice_in_dim(
        flipped, row_count - 1, row_count - 1 + row_count * (span - 1), axis=len(leading)
    )
    return picked.reshape(leading + (row_count, span - 1))[..., :count]


def relative_unshift(gradient, span):
    row_count = gradient.shape[-2]
    count = gradient.shape[-1]
    leading = gradient.shape[:-2]
    widened = jnp.pad(gradient, [(0, 0)] * len(leading) + [(0, 0), (0, span - 1 - count)])
    flat = widened.reshape(leading + (row_count * (span - 1),))
    placed = jnp.pad(flat, [(0, 0)] * len(leading) + [(row_count - 1, 1)])
    return jnp.flip(placed.reshape(leading + (row_count, span)), -1)


def matmul(left, right):
    return jnp.dot(left, right, preferred_element_type=jnp.float32)


def matmul_back(left, right):
    return lax.dot_general(
        left, right, (((1,), (1,)), ((), ())), preferred_element_type=jnp.float32
    )


def outer_sum(left, right):
    return lax.dot_general(
        left, right, (((0,), (0,)), ((), ())), preferred_element_type=jnp.float32
    )


def gate_linear(joint):
    width = joint.shape[1] // 2
    return joint[:, :width] * jax.nn.sigmoid(joint[:, width:])


def fetch_forward(local):
    return (
        lax.all_gather(local[0], ("dp", "seq"), axis=2, tiled=True),
        lax.all_gather(local[1], ("dp", "seq"), axis=1, tiled=True),
        lax.all_gather(local[2], ("dp", "seq"), axis=1, tiled=True),
        lax.all_gather(local[3], ("dp", "seq"), axis=2, tiled=True),
        lax.all_gather(local[4], ("dp", "seq"), axis=1, tiled=True),
        lax.all_gather(local[5], ("dp", "seq"), axis=1, tiled=True),
        lax.all_gather(local[6], ("dp", "seq"), axis=0, tiled=True),
        lax.all_gather(local[7], ("dp", "seq"), axis=1, tiled=True),
        lax.all_gather(local[8], ("dp", "seq"), axis=1, tiled=True),
        lax.all_gather(local[9], ("dp", "seq"), axis=1, tiled=True),
        lax.all_gather(local[10], ("dp", "seq"), axis=1, tiled=True),
    )


def fetch_backward(local):
    return (
        lax.all_gather(local[0], ("dp", "seq"), axis=2, tiled=True),
        lax.all_gather(local[1], ("dp", "seq"), axis=1, tiled=True),
        lax.all_gather(local[2], ("dp", "seq"), axis=1, tiled=True),
        lax.all_gather(local[3], ("dp", "seq"), axis=2, tiled=True),
        lax.all_gather(local[4], ("dp", "seq"), axis=1, tiled=True),
        lax.all_gather(local[5], ("dp", "seq"), axis=1, tiled=True),
        lax.all_gather(local[6], ("dp", "seq"), axis=0, tiled=True),
        lax.all_gather(local[7], ("dp", "seq"), axis=1, tiled=True),
        lax.all_gather(local[8], ("dp", "seq"), axis=1, tiled=True),
        lax.all_gather(local[9], ("dp", "seq"), axis=1, tiled=True),
        lax.all_gather(local[10], ("dp", "seq"), axis=1, tiled=True),
    )


def sum_at_end(totals):
    return (
        lax.psum_scatter(totals[0], ("dp", "seq"), scatter_dimension=2, tiled=True),
        lax.psum_scatter(totals[1], ("dp", "seq"), scatter_dimension=1, tiled=True),
        lax.psum_scatter(totals[2], ("dp", "seq"), scatter_dimension=1, tiled=True),
        lax.psum_scatter(totals[3], ("dp", "seq"), scatter_dimension=2, tiled=True),
        lax.psum_scatter(totals[4], ("dp", "seq"), scatter_dimension=1, tiled=True),
        lax.psum_scatter(totals[5], ("dp", "seq"), scatter_dimension=1, tiled=True),
        lax.psum_scatter(totals[6], ("dp", "seq"), scatter_dimension=0, tiled=True),
        lax.psum_scatter(totals[7], ("dp", "seq"), scatter_dimension=1, tiled=True),
        lax.psum_scatter(totals[8], ("dp", "seq"), scatter_dimension=1, tiled=True),
        lax.psum_scatter(totals[9], ("dp", "seq"), scatter_dimension=1, tiled=True),
        lax.psum_scatter(totals[10], ("dp", "seq"), scatter_dimension=1, tiled=True),
    )


def feed_forward(value, whole, gains_wide, biases_wide, index):
    normed_low = layer_norm(value, gains_wide[3 * index], biases_wide[3 * index]).astype(
        jnp.bfloat16
    )
    hidden = matmul(normed_low, whole[0][index]) + whole[1][index].astype(jnp.float32)
    gated_low = jax.nn.silu(hidden).astype(jnp.bfloat16)
    branch = matmul(gated_low, whole[2][index]) + biases_wide[5 + index]
    return (value + 0.5 * branch, (value, normed_low, hidden, gated_low))


def feed_backward(gradient, kept, whole, gains_wide, biases_wide, index, totals):
    value, normed_low, hidden, gated_low = kept
    branch_grad = 0.5 * gradient
    branch_low = branch_grad.astype(jnp.bfloat16)
    totals[10] = totals[10].at[5 + index].add(jnp.sum(branch_grad, 0))
    totals[2] = totals[2].at[index].add(outer_sum(gated_low, branch_low))
    gated_grad = matmul_back(branch_low, whole[2][index])
    hidden_grad = jax.vjp(jax.nn.silu, hidden)[1](gated_grad)[0]
    hidden_low = hidden_grad.astype(jnp.bfloat16)
    totals[1] = totals[1].at[index].add(jnp.sum(hidden_grad, 0))
    totals[0] = totals[0].at[index].add(outer_sum(normed_low, hidden_low))
    normed_grad = matmul_back(hidden_low, whole[0][index])
    value_grad, gain_grad, shift_grad = norm_backward(
        normed_grad, value, gains_wide[3 * index], biases_wide[3 * index]
    )
    totals[9] = totals[9].at[3 * index].add(gain_grad)
    totals[10] = totals[10].at[3 * index].add(shift_grad)
    return gradient + value_grad


def score_table(query_content, query_position, keys_all, position_rows):
    seq_count, key_count, width = keys_all.shape
    head_count = position_rows.shape[1]
    head_size = position_rows.shape[2]
    keys_heads = keys_all.reshape(seq_count, key_count, head_count, head_size)
    content = jnp.einsum(
        "sahe,sjhe->shaj", query_content, keys_heads, preferred_element_type=jnp.float32
    )
    position = jnp.einsum(
        "sahe,rhe->shar", query_position, position_rows, preferred_element_type=jnp.float32
    )
    return (content + relative_shift(position, key_count)) * head_size ** (-0.5)


def attention_forward(value, whole, gains_wide, biases_wide, valid_keys, table_low, seq_count):
    row_count, width = value.shape
    tok_count = row_count // seq_count
    head_count = width // HEAD
    heads_shape = (seq_count, tok_count, head_count, HEAD)
    normed_low = layer_norm(value, gains_wide[1], biases_wide[1]).astype(jnp.bfloat16)
    query = matmul(normed_low, whole[3][0]) + biases_wide[7]
    keys_low = (
        matmul(normed_low, whole[3][1]).astype(jnp.bfloat16).reshape(seq_count, tok_count, width)
    )
    values_low = (
        (matmul(normed_low, whole[3][2]) + biases_wide[8])
        .astype(jnp.bfloat16)
        .reshape(seq_count, tok_count, width)
    )
    query_content = (query + biases_wide[10]).astype(jnp.bfloat16).reshape(heads_shape)
    query_position = (query + biases_wide[11]).astype(jnp.bfloat16).reshape(heads_shape)
    position_rows = (
        matmul(table_low, whole[3][3]).astype(jnp.bfloat16).reshape(-1, head_count, HEAD)
    )
    keys_all, values_all = (
        lax.all_gather(keys_low, "seq", axis=1, tiled=True),
        lax.all_gather(values_low, "seq", axis=1, tiled=True),
    )
    scores = score_table(query_content, query_position, keys_all, position_rows)
    masked = jnp.where(valid_keys, scores, MASKED)
    peak = jnp.max(masked, -1, keepdims=True)
    raised = jnp.exp(masked - peak)
    total = jnp.sum(raised, -1, keepdims=True)
    probs_low = (raised / total).astype(jnp.bfloat16)
    log_total = peak + jnp.log(total)
    values_heads = values_all.reshape(seq_count, -1, head_count, HEAD)
    mixed = jnp.einsum(
        "shaj,sjhe->sahe", probs_low, values_heads, preferred_element_type=jnp.float32
    )
    mixed_low = mixed.astype(jnp.bfloat16).reshape(row_count, width)
    branch = matmul(mixed_low, whole[4]) + biases_wide[9]
    kept = (
        value,
        normed_low,
        query_content,
        query_position,
        keys_all,
        values_all,
        position_rows,
        log_total,
        mixed_low,
    )
    return (value + branch, kept)


def attention_backward(
    gradient, kept, whole, gains_wide, biases_wide, valid_keys, table_low, totals
):
    (
        value,
        normed_low,
        query_content,
        query_position,
        keys_all,
        values_all,
        position_rows,
        log_total,
        mixed_low,
    ) = kept
    seq_count, tok_count, head_count, head_size = query_content.shape
    key_count = keys_all.shape[1]
    row_count, width = value.shape
    scale = head_size ** (-0.5)
    gradient_low = gradient.astype(jnp.bfloat16)
    totals[10] = totals[10].at[9].add(jnp.sum(gradient, 0))
    totals[4] = totals[4] + outer_sum(mixed_low, gradient_low)
    mixed_grad = (
        matmul_back(gradient_low, whole[4])
        .astype(jnp.bfloat16)
        .reshape(seq_count, tok_count, head_count, head_size)
    )
    scores = score_table(query_content, query_position, keys_all, position_rows)
    probs = jnp.where(valid_keys, jnp.exp(scores - log_total), 0.0)
    values_heads = values_all.reshape(seq_count, key_count, head_count, head_size)
    keys_heads = keys_all.reshape(seq_count, key_count, head_count, head_size)
    values_grad = jnp.einsum(
        "shaj,sahe->sjhe",
        probs.astype(jnp.bfloat16),
        mixed_grad,
        preferred_element_type=jnp.float32,
    )
    probs_grad = jnp.einsum(
        "sahe,sjhe->shaj", mixed_grad, values_heads, preferred_element_type=jnp.float32
    )
    score_grad = probs * (probs_grad - jnp.sum(probs_grad * probs, -1, keepdims=True))
    score_low = score_grad.astype(jnp.bfloat16)
    content_grad = (
        jnp.einsum("shaj,sjhe->sahe", score_low, keys_heads, preferred_element_type=jnp.float32)
        * scale
    )
    keys_grad = (
        jnp.einsum("shaj,sahe->sjhe", score_low, query_content, preferred_element_type=jnp.float32)
        * scale
    )
    position_low = relative_unshift(score_low, position_rows.shape[0])
    offset_grad = (
        jnp.einsum(
            "shar,rhe->sahe", position_low, position_rows, preferred_element_type=jnp.float32
        )
        * scale
    )
    rows_grad = (
        jnp.einsum(
            "shar,sahe->rhe", position_low, query_position, preferred_element_type=jnp.float32
        )
        * scale
    )
    table_wide = table_low.astype(jnp.float32)
    totals[3] = (
        totals[3]
        .at[3]
        .add(
            lax.dot_general(
                table_wide,
                rows_grad.reshape(-1, width),
                (((0,), (0,)), ((), ())),
                precision=HIGHEST,
            )
        )
    )
    keys_sum, values_sum = (
        lax.psum_scatter(
            keys_grad.reshape(seq_count, key_count, width).astype(jnp.bfloat16),
            "seq",
            scatter_dimension=1,
            tiled=True,
        ).astype(jnp.float32),
        lax.psum_scatter(
            values_grad.reshape(seq_count, key_count, width).astype(jnp.bfloat16),
            "seq",
            scatter_dimension=1,
            tiled=True,
        ).astype(jnp.float32),
    )
    keys_sum = keys_sum.reshape(row_count, width)
    values_sum = values_sum.reshape(row_count, width)
    content_flat = content_grad.reshape(row_count, width)
    offset_flat = offset_grad.reshape(row_count, width)
    query_grad = content_flat + offset_flat
    totals[10] = totals[10].at[7].add(jnp.sum(query_grad, 0)).at[8].add(jnp.sum(values_sum, 0))
    totals[10] = totals[10].at[10].add(jnp.sum(content_flat, 0)).at[11].add(jnp.sum(offset_flat, 0))
    query_low = query_grad.astype(jnp.bfloat16)
    keys_low = keys_sum.astype(jnp.bfloat16)
    values_low = values_sum.astype(jnp.bfloat16)
    totals[3] = (
        totals[3]
        .at[0]
        .add(outer_sum(normed_low, query_low))
        .at[1]
        .add(outer_sum(normed_low, keys_low))
        .at[2]
        .add(outer_sum(normed_low, values_low))
    )
    normed_grad = (
        matmul_back(query_low, whole[3][0])
        + matmul_back(keys_low, whole[3][1])
        + matmul_back(values_low, whole[3][2])
    )
    value_grad, gain_grad, shift_grad = norm_backward(
        normed_grad, value, gains_wide[1], biases_wide[1]
    )
    totals[9] = totals[9].at[1].add(gain_grad)
    totals[10] = totals[10].at[1].add(shift_grad)
    return gradient + value_grad


def convolution_forward(value, whole, gains_wide, biases_wide, valid, valid_total, seq_count):
    row_count, width = value.shape
    tok_count = row_count // seq_count
    kernel_size = whole[7].shape[0]
    half = kernel_size // 2
    normed_low = layer_norm(value, gains_wide[2], biases_wide[2]).astype(jnp.bfloat16)
    joint = matmul(normed_low, whole[5]) + whole[6].astype(jnp.float32)
    gated_low = (gate_linear(joint).reshape(seq_count, tok_count, width) * valid).astype(
        jnp.bfloat16
    )
    extended = with_halo(gated_low, (("seq", 1),), half)
    extended_wide = extended.astype(jnp.float32)
    kernel = whole[7].astype(jnp.float32)
    filtered = extended_wide[:, 0:tok_count, :] * kernel[0]
    for offset in range(1, kernel_size):
        filtered = filtered + extended_wide[:, offset : offset + tok_count, :] * kernel[offset]
    center = lax.psum(jnp.sum(filtered * valid, (0, 1)), ("dp", "seq")) / valid_total
    spread = (filtered - center) * valid
    variance = lax.psum(jnp.sum(spread * spread, (0, 1)), ("dp", "seq")) / valid_total
    reciprocal = lax.rsqrt(variance + EPSILON)
    standard = (filtered - center) * reciprocal
    shaped = standard * gains_wide[5] + biases_wide[13]
    swished_low = jax.nn.silu(shaped).astype(jnp.bfloat16).reshape(row_count, width)
    branch = matmul(swished_low, whole[8]) + biases_wide[12]
    return (
        value + branch,
        (value, normed_low, joint, extended, standard, reciprocal, shaped, swished_low),
    )


def convolution_backward(
    gradient, kept, whole, gains_wide, biases_wide, valid, valid_total, totals
):
    value, normed_low, joint, extended, standard, reciprocal, shaped, swished_low = kept
    seq_count, tok_count, width = standard.shape
    row_count = seq_count * tok_count
    kernel_size = whole[7].shape[0]
    half = kernel_size // 2
    gradient_low = gradient.astype(jnp.bfloat16)
    totals[10] = totals[10].at[12].add(jnp.sum(gradient, 0))
    totals[8] = totals[8] + outer_sum(swished_low, gradient_low)
    swished_grad = matmul_back(gradient_low, whole[8]).reshape(seq_count, tok_count, width)
    shaped_grad = jax.vjp(jax.nn.silu, shaped)[1](swished_grad)[0]
    beta_local = jnp.sum(shaped_grad, (0, 1))
    gamma_local = jnp.sum(shaped_grad * standard, (0, 1))
    totals[9] = totals[9].at[5].add(gamma_local)
    totals[10] = totals[10].at[13].add(beta_local)
    beta_all, gamma_all = lax.psum((beta_local, gamma_local), ("dp", "seq"))
    filtered_grad = (
        reciprocal
        * gains_wide[5]
        * (shaped_grad - valid * (beta_all + standard * gamma_all) / valid_total)
    )
    filtered_low = filtered_grad.astype(jnp.bfloat16)
    extended_wide = extended.astype(jnp.float32)
    filtered_wide = filtered_low.astype(jnp.float32)
    kernel_grad = jnp.stack(
        [
            jnp.sum(extended_wide[:, offset : offset + tok_count, :] * filtered_wide, (0, 1))
            for offset in range(kernel_size)
        ]
    )
    totals[7] = totals[7] + kernel_grad
    rim = with_halo(filtered_low, (("seq", 1),), half)
    rim_wide = rim.astype(jnp.float32)
    kernel = whole[7].astype(jnp.float32)
    gated_grad = rim_wide[:, 2 * half : 2 * half + tok_count, :] * kernel[0]
    for offset in range(1, kernel_size):
        gated_grad = (
            gated_grad
            + rim_wide[:, 2 * half - offset : 2 * half - offset + tok_count, :] * kernel[offset]
        )
    glu_grad = (gated_grad * valid).reshape(row_count, width)
    joint_grad = jax.vjp(gate_linear, joint)[1](glu_grad)[0]
    joint_low = joint_grad.astype(jnp.bfloat16)
    totals[6] = totals[6] + jnp.sum(joint_grad, 0)
    totals[5] = totals[5] + outer_sum(normed_low, joint_low)
    normed_grad = matmul_back(joint_low, whole[5])
    value_grad, gain_grad, shift_grad = norm_backward(
        normed_grad, value, gains_wide[2], biases_wide[2]
    )
    totals[9] = totals[9].at[2].add(gain_grad)
    totals[10] = totals[10].at[2].add(shift_grad)
    return gradient + value_grad


def body(
    inputs,
    lengths,
    cotangent,
    feed_in,
    feed_in_bias,
    feed_out,
    attend_in,
    attend_out,
    point_in,
    point_in_bias,
    depth_kernel,
    point_out,
    gains,
    biases,
):
    local = (
        feed_in,
        feed_in_bias,
        feed_out,
        attend_in,
        attend_out,
        point_in,
        point_in_bias,
        depth_kernel,
        point_out,
        gains,
        biases,
    )
    micro_count, seq_count, tok_count, width = inputs.shape
    seq_len = tok_count * lax.axis_size("seq")
    valid_total = seq_count * lax.axis_size("dp") * seq_len * 3 // 4
    first = lax.axis_index("seq") * tok_count
    positions = first + jnp.arange(tok_count, dtype=jnp.int32)
    offsets = first - seq_len + 1 + jnp.arange(seq_len + tok_count - 1, dtype=jnp.int32)
    table_low = sinusoid(offsets, width).astype(jnp.bfloat16)
    key_places = jnp.arange(seq_len, dtype=jnp.int32)
    layer_outs = []
    input_grads = []
    totals = None
    shards = None
    for micro in range(micro_count):
        whole = fetch_forward(local)
        if totals is None:
            totals = [jnp.zeros(array.shape, jnp.float32) for array in whole]
        gains_wide = whole[9].astype(jnp.float32)
        biases_wide = whole[10].astype(jnp.float32)
        lengths_now = lengths[micro]
        valid = (positions[None, :] < lengths_now[:, None]).astype(jnp.float32)[:, :, None]
        valid_keys = (key_places[None, :] < lengths_now[:, None])[:, None, None, :]
        start_value = inputs[micro].astype(jnp.float32).reshape(seq_count * tok_count, width)
        first_value, first_kept = feed_forward(start_value, whole, gains_wide, biases_wide, 0)
        second_value, second_kept = attention_forward(
            first_value, whole, gains_wide, biases_wide, valid_keys, table_low, seq_count
        )
        third_value, third_kept = convolution_forward(
            second_value, whole, gains_wide, biases_wide, valid, valid_total, seq_count
        )
        fourth_value, fourth_kept = feed_forward(third_value, whole, gains_wide, biases_wide, 1)
        final = layer_norm(fourth_value, gains_wide[4], biases_wide[4])
        layer_outs.append(final.astype(jnp.bfloat16).reshape(seq_count, tok_count, width))
        whole = fetch_backward(local)
        gradient = cotangent[micro].astype(jnp.float32).reshape(seq_count * tok_count, width)
        gradient, gain_grad, shift_grad = norm_backward(
            gradient, fourth_value, gains_wide[4], biases_wide[4]
        )
        totals[9] = totals[9].at[4].add(gain_grad)
        totals[10] = totals[10].at[4].add(shift_grad)
        gradient = feed_backward(gradient, fourth_kept, whole, gains_wide, biases_wide, 1, totals)
        gradient = convolution_backward(
            gradient, third_kept, whole, gains_wide, biases_wide, valid, valid_total, totals
        )
        gradient = attention_backward(
            gradient, second_kept, whole, gains_wide, biases_wide, valid_keys, table_low, totals
        )
        gradient = feed_backward(gradient, first_kept, whole, gains_wide, biases_wide, 0, totals)
        input_grads.append(gradient.reshape(seq_count, tok_count, width))
    shards = sum_at_end(totals)
    return (
        jnp.stack(layer_outs),
        jnp.stack(input_grads),
        shards[0],
        shards[1],
        shards[2],
        shards[3],
        shards[4],
        shards[5],
        shards[6],
        shards[7],
        shards[8],
        shards[9],
        shards[10],
    )


def solution(mesh):
    placed = (
        P(None, "dp", "seq", None),
        P(None, "dp"),
        P(None, "dp", "seq", None),
        P(None, None, ("dp", "seq")),
        P(None, ("dp", "seq")),
        P(None, ("dp", "seq"), None),
        P(None, None, ("dp", "seq")),
        P(None, ("dp", "seq")),
        P(None, ("dp", "seq")),
        P(("dp", "seq")),
        P(None, ("dp", "seq")),
        P(None, ("dp", "seq")),
        P(None, ("dp", "seq")),
        P(None, ("dp", "seq")),
    )
    return jax.shard_map(
        body,
        mesh=mesh,
        in_specs=placed,
        out_specs=(
            P(None, "dp", "seq", None),
            P(None, "dp", "seq", None),
            P(None, None, ("dp", "seq")),
            P(None, ("dp", "seq")),
            P(None, ("dp", "seq"), None),
            P(None, None, ("dp", "seq")),
            P(None, ("dp", "seq")),
            P(None, ("dp", "seq")),
            P(("dp", "seq")),
            P(None, ("dp", "seq")),
            P(None, ("dp", "seq")),
            P(None, ("dp", "seq")),
            P(None, ("dp", "seq")),
        ),
        check_vma=False,
    )
```

profile of v0, /device:TPU:0, one launch (start us, length us, event | category | flops | bytes accessed | tf_op | source)
XLA Modules:
  0.0 2206.6 jit_solution(8635185823224071009)
XLA Ops:
  8.7 70.4 %all_gather.81 = bf16[31,256]{0,1:T(8,128)(2,1)S(1)} all-gather(bf16[31,8]{0,1:T(8,128)(2,1)} %param.144), channel_id=1, replica_groups=mesh['dp'=16,'seq'=2] {'dp','seq'}, dimensions={1}, use_global_device_ids=true | all-gather | bytes 16368 | tf_op jit(solution)/shard_map/all_gather | solution.py:104
  86.6 37.0 %all-reduce.11 = bf16[512]{0:T(512)(128)(2,1)S(1)} all-reduce(bf16[512]{0:T(512)(128)(2,1)S(1)} %dynamic-update-slice.180), channel_id=1, replica_groups=mesh['dp'=16,'seq'=2] {'dp','seq'}, use_global_device_ids=true, to_apply=%add.11 | all-reduce | flops 512 | bytes 2048
  124.3 66.0 %all-gather.4 = bf16[32,32,2]{1,2,0:T(2,128)(2,1)S(1)} all-gather(bf16[1,32,2]{1,2,0:T(2,128)(2,1)S(1)} %bitcast.866), channel_id=1, replica_groups=mesh['dp'=16,'seq'=2] {'dp','seq'}, dimensions={0}, use_global_device_ids=true | all-gather | bytes 4224 | tf_op jit(solution)/shard_map/all_gather | solution.py:98
  190.4 63.7 %all_gather.30 = bf16[6,256]{0,1:T(8,128)(2,1)S(1)} all-gather(bf16[6,8]{0,1:T(8,128)(2,1)S(1)} %copy.141), channel_id=1, replica_groups=mesh['dp'=16,'seq'=2] {'dp','seq'}, dimensions={1}, use_global_device_ids=true | all-gather | bytes 3168 | tf_op jit(solution)/shard_map/all_gather | solution.py:106
  255.1 65.9 %all_gather.31 = bf16[14,256]{0,1:T(8,128)(2,1)S(1)} all-gather(bf16[14,8]{0,1:T(8,128)(2,1)S(1)} %copy-done.325), channel_id=1, replica_groups=mesh['dp'=16,'seq'=2] {'dp','seq'}, dimensions={1}, use_global_device_ids=true | all-gather | bytes 7392 | tf_op jit(solution)/shard_map/all_gather | solution.py:107
  322.6 64.0 %all_gather.38 = bf16[256,256]{0,1:T(8,128)(2,1)S(1)} all-gather(bf16[256,8]{0,1:T(8,128)(2,1)S(1)} %copy-done.305), channel_id=1, replica_groups=mesh['dp'=16,'seq'=2] {'dp','seq'}, dimensions={1}, use_global_device_ids=true | all-gather | bytes 135168 | tf_op jit(solution)/shard_map/all_gather | solution.py:101
  386.6 71.1 %all_gather.82 = bf16[256,256]{0,1:T(8,128)(2,1)} all-gather(bf16[256,8]{0,1:T(8,128)(2,1)S(1)} %copy-done.306), channel_id=1, replica_groups=mesh['dp'=16,'seq'=2] {'dp','seq'}, dimensions={1}, use_global_device_ids=true | all-gather | bytes 135168 | tf_op jit(solution)/shard_map/all_gather | solution.py:105
  457.7 64.8 %all_gather.39 = bf16[256,512]{0,1:T(8,128)(2,1)S(1)} all-gather(bf16[256,16]{0,1:T(8,128)(2,1)S(1)} %copy-done.274), channel_id=1, replica_groups=mesh['dp'=16,'seq'=2] {'dp','seq'}, dimensions={1}, use_global_device_ids=true | all-gather | bytes 270336 | tf_op jit(solution)/shard_map/all_gather | solution.py:102
  524.4 68.3 %all_gather.35 = bf16[4,256,256]{1,2,0:T(8,128)(2,1)S(1)} all-gather(bf16[4,256,8]{1,2,0:T(8,128)(2,1)S(1)} %copy-done.260), channel_id=1, replica_groups=mesh['dp'=16,'seq'=2] {'dp','seq'}, dimensions={2}, use_global_device_ids=true | all-gather | bytes 540672 | tf_op jit(solution)/shard_map/all_gather | solution.py:100
  606.3 6.3 all-gather.1
  613.5 7.4 all-gather.2
  621.9 8.5 all-gather
  631.3 6.6 all-gather.3
  640.3 4.1 convolution_bitcast_fusion
  644.4 56.0 %rev.17 = f32[1,4,384,1151]{2,3,1,0:T(8,128)} reverse(f32[1,4,384,1151]{2,3,1,0:T(8,128)} %convolution_bitcast_fusion), dimensions={3} | reverse | bytes 14143488 | tf_op jit(solution)/shard_map/jit(_flip)/rev | solution.py:57
  700.5 8.1 copy.150
  708.5 12.8 reshape.2651
  721.3 8.4 slice.2254
  729.8 15.4 reshape.2652
  753.9 3.5 collective-permute-start.2
  759.1 4.1 convolution_bitcast_fusion.1
  763.2 56.0 %rev.16 = f32[1,4,384,1151]{2,3,1,0:T(8,128)} reverse(f32[1,4,384,1151]{2,3,1,0:T(8,128)} %convolution_bitcast_fusion.1), dimensions={3} | reverse | bytes 14143488 | tf_op jit(solution)/shard_map/jit(_flip)/rev | solution.py:57
  819.3 8.1 copy.145
  827.3 12.8 reshape.2640
  840.1 8.4 slice.2172
  848.6 15.4 reshape.2641
  864.0 3.3 select_reduce_fusion.1
  873.0 4.5 collective-permute-start
  884.3 36.9 %all-reduce.21 = (f32[256]{0:T(256)}, f32[256]{0:T(256)}) all-reduce(f32[256]{0:T(256)S(1)} %get-tuple-element.973, f32[256]{0:T(256)S(1)} %get-tuple-element.971), channel_id=1, replica_groups=mesh['dp'=16,'seq'=2] {'dp','seq'}, use_global_device_ids=true, to_apply=%region_25.26 | all-reduce | flops 512 | bytes 4096 | tf_op jit(solution)/shard_map/psum | solution.py:375
  923.3 42.4 %all-reduce.20 = (f32[256]{0:T(256)S(1)}, f32[256]{0:T(256)S(1)}) all-reduce(f32[256]{0:T(256)} %multiply_reduce_fusion.16, f32[256]{0:T(256)S(1)} %multiply_reduce_fusion.22), channel_id=1, replica_groups=mesh['dp'=16,'seq'=2] {'dp','seq'}, use_global_device_ids=true, to_apply=%region_27.28 | all-reduce | flops 512 | bytes 4096 | tf_op jit(solution)/shard_map/psum | solution.py:377
  999.8 39.0 %all-reduce.19 = (f32[256]{0:T(256)S(1)}, f32[256]{0:T(256)S(1)}, f32[256]{0:T(256)}, f32[256]{0:T(256)}) all-reduce(f32[256]{0:T(256)S(1)} %get-tuple-element.880, f32[256]{0:T(256)S(1)} %get-tuple-element.879, f32[256]{0:T(256)S(1)} %get-tuple-element.878, ...), channel_id=1, replica_groups=mesh['dp'=16,'seq'=2] {'dp','seq'}, use_global_device_ids=true, to_apply=%region_56.57 | all-reduce | flops 1024 | bytes 8192 | tf_op jit(solution)/shard_map/psum | solution.py:406
  1045.1 4.8 collective-permute-start.4
  1056.3 5.1 collective-permute-start.6
  1078.2 4.2 fusion.76
  1082.4 6.0 fusion.5
  1089.7 3.7 fusion.3
  1095.1 4.4 fusion.4
  1101.6 7.7 reshape.2815
  1109.2 5.1 reshape.2660
  1114.3 5.5 pad.155
  1119.8 6.2 reshape.2817
  1126.0 10.0 reshape.2661
  1136.1 53.3 %reverse.1 = bf16[1,4,384,1152]{3,2,1,0:T(8,128)(2,1)} reverse(bf16[1,4,384,1152]{3,2,1,0:T(8,128)(2,1)} %bitcast.708), dimensions={3} | reverse | bytes 7077888
  1189.4 4.3 fusion.18
  1193.7 5.4 fusion.2
  1222.0 7.8 reshape.2811
  1229.8 5.1 reshape.2668
  1234.9 5.5 pad.159
  1240.4 6.3 reshape.2813
  1246.7 9.6 reshape.2669
  1256.3 53.3 %reverse = bf16[1,4,384,1152]{3,2,1,0:T(8,128)(2,1)} reverse(bf16[1,4,384,1152]{3,2,1,0:T(8,128)(2,1)} %bitcast.709), dimensions={3} | reverse | bytes 7077888
  1312.2 4.6 fusion.446
  1320.8 4.5 fusion.444
  1332.4 9.3 reduce-scatter.31.cloned.1.call-done
  1348.8 8.2 reduce-scatter.35.cloned.1.call-done
  1403.7 5.3 stack.263
  1409.0 5.3 stack.231
  1451.0 39.9 %all-reduce.18 = (f32[512]{0:T(512)S(1)}, f32[31,256]{1,0:T(8,128)S(1)}, f32[6,256]{1,0:T(8,128)S(1)}, f32[14,256]{1,0:T(8,128)S(1)}) all-reduce(f32[512]{0:T(512)S(1)} %copy-done.275, f32[31,256]{1,0:T(8,128)S(1)} %copy-done.131, f32[6,256]{1,0:T(8,128)S(1)} %scatter-add.236, ...), channel_id=16, replica_groups=mesh['dp'=16,'seq'=2] {'dp','seq'}, use_global_device_ids=true, to_apply=%region_78.79.clone | all-reduce | flops 13568 | bytes 108544
  1493.7 22.6 %reduce-scatter.39.cloned.1.call-done = f32[32,2]{1,0:T(8,128)} async-done(((f32[1024,2]{1,0:T(8,128)}), f32[32,2]{1,0:T(8,128)}) %reduce-scatter.39.cloned.1.call-update) | async-done | bytes 272
  1517.7 138.3 %all-reduce.25.cloned.1.call-done = (f32[2,256,1024]{1,0,2:T(2,128)}, f32[4,256,256]{1,0,2:T(4,128)}) async-done(((f32[2,256,1024]{1,0,2:T(2,128)}, f32[4,256,256]{1,0,2:T(4,128)}), (f32[2,256,1024]{1,0,2:T(2,128)}, f32[4,256,256]{1,0,2:T(4,128)})) %all-reduce.25.cloned.1.call-update) | async-done | bytes 3145744
  1658.9 134.6 %reduce-scatter.29.cloned.1.call-done = f32[256,8]{0,1:T(8,128)} async-done(((f32[256,256]{0,1:T(8,128)}), f32[256,8]{0,1:T(8,128)}) %reduce-scatter.29.cloned.1.call-update) | async-done | bytes 8208 | tf_op jit(solution)/shard_map/reduce_scatter | solution.py:137
  1793.5 134.2 %reduce-scatter.25.cloned.1.call-done = f32[256,8]{0,1:T(8,128)} async-done(((f32[256,256]{0,1:T(8,128)}), f32[256,8]{0,1:T(8,128)}) %reduce-scatter.25.cloned.1.call-update) | async-done | bytes 8208 | tf_op jit(solution)/shard_map/reduce_scatter | solution.py:133
  1927.7 134.5 %reduce-scatter.27.cloned.1.call-done = f32[256,16]{0,1:T(8,128)} async-done(((f32[256,512]{0,1:T(8,128)}), f32[256,16]{0,1:T(8,128)}) %reduce-scatter.27.cloned.1.call-update) | async-done | bytes 16400 | tf_op jit(solution)/shard_map/reduce_scatter | solution.py:134
  2062.2 137.4 %reduce-scatter.23.cloned.1.call-done = f32[2,32,256]{2,1,0:T(8,128)} async-done(((f32[2,1024,256]{2,1,0:T(8,128)}), f32[2,32,256]{2,1,0:T(8,128)}) %reduce-scatter.23.cloned.1.call-update) | async-done | bytes 65552 | tf_op jit(solution)/shard_map/reduce_scatter | solution.py:131
  (1065 shorter events, 256.0 us)
Async XLA Ops:
  7.2 588.5 %all-gather.8.cloned.1.call-start = ((), (), s32[]{:S(2)}) async-start(), calls=%async_computation.9 | async-start | bytes 1081344 | tf_op jit(solution)/shard_map/all_gather | solution.py:97
  7.9 590.7 %all-gather.10.cloned.1.call-start = ((), (), s32[]{:S(2)}) async-start(), calls=%async_computation.10 | async-start | bytes 1081344 | tf_op jit(solution)/shard_map/all_gather | solution.py:99
  8.7 1320.2 %reduce-scatter.37.cloned.1.call-start = ((), (), s32[]{:S(2)}) async-start(), calls=%async_computation.18 | async-start | bytes 589824
  79.1 45.1 %copy-start.326 = (bf16[6,8]{1,0:T(8,128)(2,1)S(1)}, bf16[6,8]{1,0:T(8,128)(2,1)}, u32[]{:S(2)}) copy-start(bf16[6,8]{1,0:T(8,128)(2,1)} %param.146) | copy-start | bytes 292
  79.1 45.2 %copy-start.334 = (bf16[2,32]{1,0:T(2,128)(2,1)S(1)}, bf16[2,32]{1,0:T(2,128)(2,1)}, u32[]{:S(2)}) copy-start(bf16[2,32]{1,0:T(2,128)(2,1)} %param.138) | copy-start | bytes 388
  80.7 174.4 %copy-start.325 = (bf16[14,8]{0,1:T(8,128)(2,1)S(1)}, bf16[14,8]{0,1:T(8,128)(2,1)}, u32[]{:S(2)}) copy-start(bf16[14,8]{0,1:T(8,128)(2,1)} %param.147) | copy-start | bytes 676
  82.6 239.9 %copy-start.305 = (bf16[256,8]{0,1:T(8,128)(2,1)S(1)}, bf16[256,8]{0,1:T(8,128)(2,1)}, u32[]{:S(2)}) copy-start(bf16[256,8]{0,1:T(8,128)(2,1)} %param.141) | copy-start | bytes 12292
  82.6 304.0 %copy-start.306 = (bf16[256,8]{0,1:T(8,128)(2,1)S(1)}, bf16[256,8]{0,1:T(8,128)(2,1)}, u32[]{:S(2)}) copy-start(bf16[256,8]{0,1:T(8,128)(2,1)} %param.145) | copy-start | bytes 12292
  82.6 375.1 %copy-start.274 = (bf16[256,16]{0,1:T(8,128)(2,1)S(1)}, bf16[256,16]{0,1:T(8,128)(2,1)}, u32[]{:S(2)}) copy-start(bf16[256,16]{0,1:T(8,128)(2,1)} %param.142) | copy-start | bytes 24580
  82.6 439.8 %copy-start.128 = (bf16[2,1,384,256]{3,2,1,0:T(8,128)(2,1)S(1)}, bf16[2,1,384,256]{3,2,1,0:T(8,128)(2,1)}, u32[]{:S(2)}) copy-start(bf16[2,1,384,256]{3,2,1,0:T(8,128)(2,1)} %param.134) | copy-start | bytes 1179652
  85.0 664.6 %copy-start.174 = (pred[768]{0:T(1024)(128)(4,1)}, pred[768]{0:T(1024)(128)(4,1)S(1)}, u32[]{:S(2)}) copy-start(pred[768]{0:T(1024)(128)(4,1)S(1)} %iota_compare_fusion) | copy-start | bytes 2308
  255.1 345.9 %copy-start.151 = (f32[256]{0:T(256)}, f32[256]{0:T(256)S(1)}, u32[]{:S(2)}) copy-start(f32[256]{0:T(256)S(1)} %get-tuple-element.886) | copy-start | bytes 3076
  255.1 348.6 %copy-start.169 = (f32[256]{0:T(256)}, f32[256]{0:T(256)S(1)}, u32[]{:S(2)}) copy-start(f32[256]{0:T(256)S(1)} %get-tuple-element.885) | copy-start | bytes 3076
  255.1 740.5 %copy-start.142 = (f32[256]{0:T(256)}, f32[256]{0:T(256)S(1)}, u32[]{:S(2)}) copy-start(f32[256]{0:T(256)S(1)} %get-tuple-element.882) | copy-start | bytes 3076
  321.0 202.2 %copy-start.129 = (bf16[2,1,384,256]{3,2,1,0:T(8,128)(2,1)S(1)}, bf16[2,1,384,256]{3,2,1,0:T(8,128)(2,1)}, u32[]{:S(2)}) copy-start(bf16[2,1,384,256]{3,2,1,0:T(8,128)(2,1)} %param.136) | copy-start | bytes 1179652
  322.5 278.4 %copy-start.257 = (f32[256]{0:T(256)}, f32[256]{0:T(256)S(1)}, u32[]{:S(2)}) copy-start(f32[256]{0:T(256)S(1)} %get-tuple-element.900) | copy-start | bytes 3076
  322.6 429.7 %copy-start.263 = (f32[256]{0:T(256)}, f32[256]{0:T(256)S(1)}, u32[]{:S(2)}) copy-start(f32[256]{0:T(256)S(1)} %get-tuple-element.893) | copy-start | bytes 3076
  386.6 484.5 %copy-start.58 = (bf16[256,256]{0,1:T(8,128)(2,1)}, bf16[256,256]{0,1:T(8,128)(2,1)S(1)}, u32[]{:S(2)}) copy-start(bf16[256,256]{0,1:T(8,128)(2,1)S(1)} %all_gather.38) | copy-start | bytes 393220
  522.7 80.3 %copy-start.19 = (bf16[1,1,384,256]{2,3,1,0:T(8,128)(2,1)}, bf16[1,1,384,256]{2,3,1,0:T(8,128)(2,1)S(1)}, u32[]{:S(2)}) copy-start(bf16[1,1,384,256]{2,3,1,0:T(8,128)(2,1)S(1)} %copy.208) | copy-start | bytes 589828
  522.7 78.2 %copy-start.144 = (f32[384]{0:T(512)}, f32[384]{0:T(512)S(1)}, u32[]{:S(2)}) copy-start(f32[384]{0:T(512)S(1)} %broadcast_multiply_fusion.9) | copy-start | bytes 4612
  523.0 75.6 %copy-start.15 = (bf16[1,1,384,256]{2,3,1,0:T(8,128)(2,1)}, bf16[1,1,384,256]{2,3,1,0:T(8,128)(2,1)S(1)}, u32[]{:S(2)}) copy-start(bf16[1,1,384,256]{2,3,1,0:T(8,128)(2,1)S(1)} %copy.209) | copy-start | bytes 589828
  523.1 72.6 %copy-start.136 = (f32[384]{0:T(512)}, f32[384]{0:T(512)S(1)}, u32[]{:S(2)}) copy-start(f32[384]{0:T(512)S(1)} %broadcast_multiply_fusion.4) | copy-start | bytes 4612
  523.4 75.2 %copy-start.65 = (bf16[1,1,384,256]{2,3,1,0:T(8,128)(2,1)}, bf16[1,1,384,256]{2,3,1,0:T(8,128)(2,1)S(1)}, u32[]{:S(2)}) copy-start(bf16[1,1,384,256]{2,3,1,0:T(8,128)(2,1)S(1)} %copy.210) | copy-start | bytes 589828
  523.7 74.9 %copy-start.67 = (bf16[1,1,384,256]{2,3,1,0:T(8,128)(2,1)}, bf16[1,1,384,256]{2,3,1,0:T(8,128)(2,1)S(1)}, u32[]{:S(2)}) copy-start(bf16[1,1,384,256]{2,3,1,0:T(8,128)(2,1)S(1)} %copy.211) | copy-start | bytes 589828
  524.4 76.6 %copy-start.162 = (f32[384]{0:T(512)}, f32[384]{0:T(512)S(1)}, u32[]{:S(2)}) copy-start(f32[384]{0:T(512)S(1)} %fusion.404) | copy-start | bytes 4612
  524.4 74.2 %copy-start.157 = (f32[384]{0:T(512)}, f32[384]{0:T(512)S(1)}, u32[]{:S(2)}) copy-start(f32[384]{0:T(512)S(1)} %fusion.409) | copy-start | bytes 4612
  592.8 46.6 %copy-start.26 = (bf16[4,256,256]{1,2,0:T(8,128)(2,1)}, bf16[4,256,256]{1,2,0:T(8,128)(2,1)S(1)}, u32[]{:S(2)}) copy-start(bf16[4,256,256]{1,2,0:T(8,128)(2,1)S(1)} %all_gather.35) | copy-start | bytes 1572868
  595.6 44.7 %copy-start.76 = (bf16[1151,256]{0,1:T(8,128)(2,1)}, bf16[1151,256]{0,1:T(8,128)(2,1)S(1)}, u32[]{:S(2)}) copy-start(bf16[1151,256]{0,1:T(8,128)(2,1)S(1)} %convolution_convert_fusion) | copy-start | bytes 1767940
  600.9 151.3 %copy-start.9 = (f32[384,256]{0,1:T(8,128)}, f32[384,256]{0,1:T(8,128)S(1)}, u32[]{:S(2)}) copy-start(f32[384,256]{0,1:T(8,128)S(1)} %get-tuple-element.1033) | copy-start | bytes 1179652
  603.4 267.6 %copy-start.11 = (f32[384,256]{0,1:T(8,128)}, f32[384,256]{0,1:T(8,128)S(1)}, u32[]{:S(2)}) copy-start(f32[384,256]{0,1:T(8,128)S(1)} %get-tuple-element.1031) | copy-start | bytes 1179652
  639.1 106.2 %copy-start.55 = (bf16[768,256]{0,1:T(8,128)(2,1)}, bf16[768,256]{0,1:T(8,128)(2,1)S(1)}, u32[]{:S(2)}) copy-start(bf16[768,256]{0,1:T(8,128)(2,1)S(1)} %copy.149) | copy-start | bytes 1179652
  640.3 118.8 %copy-start.85 = (bf16[384,256]{0,1:T(8,128)(2,1)}, bf16[384,256]{0,1:T(8,128)(2,1)S(1)}, u32[]{:S(2)}) copy-start(bf16[384,256]{0,1:T(8,128)(2,1)S(1)} %get-tuple-element.1001) | copy-start | bytes 589828
  752.5 322.8 %copy-start.4 = (f32[384,256]{0,1:T(8,128)}, f32[384,256]{0,1:T(8,128)S(1)}, u32[]{:S(2)}) copy-start(f32[384,256]{0,1:T(8,128)S(1)} %get-tuple-element.1041) | copy-start | bytes 1179652
  752.5 322.8 %copy-start.134 = (f32[384]{0:T(512)}, f32[384]{0:T(512)S(1)}, u32[]{:S(2)}) copy-start(f32[384]{0:T(512)S(1)} %broadcast_multiply_fusion.2) | copy-start | bytes 4612
  752.6 322.7 %copy-start.155 = (f32[384]{0:T(512)}, f32[384]{0:T(512)S(1)}, u32[]{:S(2)}) copy-start(f32[384]{0:T(512)S(1)} %fusion.411) | copy-start | bytes 4612
  753.9 125.4 %collective-permute-start.2 = (bf16[1,15,256]{2,1,0:T(8,128)(2,1)S(1)}, bf16[1,15,256]{2,1,0:T(8,128)(2,1)S(1)}, u32[]{:S(2)}, u32[]{:S(2)}) collective-permute-start(bf16[1,15,256]{2,1,0:T(8,128)(2,1)S(1)} %get-tuple-element.995), channel_id=1, source_target_pairs={{0,1},{2,3},{4,5},{6,7},{8,9},{10,11},{12,13},{14,15},{16,17},{18,... | collective-permute-start | bytes 23048 | tf_op jit(solution)/shard_map/ppermute | solution.py:24
  757.4 121.9 %collective-permute-start.3 = (bf16[1,15,256]{2,1,0:T(8,128)(2,1)S(1)}, bf16[1,15,256]{2,1,0:T(8,128)(2,1)S(1)}, u32[]{:S(2)}, u32[]{:S(2)}) collective-permute-start(bf16[1,15,256]{2,1,0:T(8,128)(2,1)S(1)} %get-tuple-element.996), channel_id=1, source_target_pairs={{1,0},{3,2},{5,4},{7,6},{9,8},{11,10},{13,12},{15,14},{17,16},{19,... | collective-permute-start | bytes 23048 | tf_op jit(solution)/shard_map/ppermute | solution.py:26
  871.6 203.7 %copy-start.6 = (f32[384,256]{0,1:T(8,128)}, f32[384,256]{0,1:T(8,128)S(1)}, u32[]{:S(2)}) copy-start(f32[384,256]{0,1:T(8,128)S(1)} %get-tuple-element.1037) | copy-start | bytes 1179652
  871.6 203.7 %copy-start.135 = (f32[384]{0:T(512)}, f32[384]{0:T(512)S(1)}, u32[]{:S(2)}) copy-start(f32[384]{0:T(512)S(1)} %broadcast_multiply_fusion.7) | copy-start | bytes 4612
  871.7 203.6 %copy-start.156 = (f32[384]{0:T(512)}, f32[384]{0:T(512)S(1)}, u32[]{:S(2)}) copy-start(f32[384]{0:T(512)S(1)} %fusion.406) | copy-start | bytes 4612
  873.0 8.5 collective-permute-start
  877.6 5.5 collective-permute-start.1
  883.2 82.5 %copy-start.288 = (f32[256]{0:T(256)S(1)}, f32[256]{0:T(256)}, u32[]{:S(2)}) copy-start(f32[256]{0:T(256)} %get-tuple-element.883) | copy-start | bytes 3076
  884.3 83.4 %copy-start.48 = (f32[1,384,256]{2,1,0:T(8,128)}, f32[1,384,256]{2,1,0:T(8,128)S(1)}, u32[]{:S(2)}) copy-start(f32[1,384,256]{2,1,0:T(8,128)S(1)} %get-tuple-element.972) | copy-start | bytes 1179652
  921.8 47.4 %copy-start.265 = (f32[256]{0:T(256)}, f32[256]{0:T(256)S(1)}, u32[]{:S(2)}) copy-start(f32[256]{0:T(256)S(1)} %broadcast_multiply_fusion.10) | copy-start | bytes 3076
  922.5 45.1 %copy-start.268 = (f32[256]{0:T(256)}, f32[256]{0:T(256)S(1)}, u32[]{:S(2)}) copy-start(f32[256]{0:T(256)S(1)} %broadcast_multiply_fusion.11) | copy-start | bytes 3076
  998.6 40.2 %copy-start.320 = (f32[256]{0:T(256)}, f32[256]{0:T(256)S(1)}, u32[]{:S(2)}) copy-start(f32[256]{0:T(256)S(1)} %get-tuple-element.878) | copy-start | bytes 3076
  998.6 42.8 %copy-start.318 = (f32[256]{0:T(256)}, f32[256]{0:T(256)S(1)}, u32[]{:S(2)}) copy-start(f32[256]{0:T(256)S(1)} %get-tuple-element.877) | copy-start | bytes 3076
  999.8 41.7 %copy-start.314 = (f32[256]{0:T(256)}, f32[256]{0:T(256)S(1)}, u32[]{:S(2)}) copy-start(f32[256]{0:T(256)S(1)} %get-tuple-element.880) | copy-start | bytes 3076
  999.8 41.7 %copy-start.316 = (f32[256]{0:T(256)}, f32[256]{0:T(256)S(1)}, u32[]{:S(2)}) copy-start(f32[256]{0:T(256)S(1)} %get-tuple-element.879) | copy-start | bytes 3076
  1045.1 18.9 collective-permute-start.4
  1049.8 14.2 collective-permute-start.5
  1056.3 11.3 collective-permute-start.6
  1061.4 6.2 collective-permute-start.7
  1094.8 235.8 %reduce-scatter.33.cloned.1.call-start = ((), (), s32[]{:S(2)}) async-start(), calls=%async_computation.16 | async-start | bytes 589824
  1136.1 53.3 %copy-start.86 = (bf16[384,256]{0,1:T(8,128)(2,1)S(1)}, bf16[384,256]{0,1:T(8,128)(2,1)}, u32[]{:S(2)}) copy-start(bf16[384,256]{0,1:T(8,128)(2,1)} %copy-done.85) | copy-start | bytes 589828
  1312.2 29.5 %reduce-scatter.31.cloned.1.call-start = ((), (), s32[]{:S(2)}) async-start(), calls=%async_computation.15 | async-start | bytes 589824
  1320.3 36.7 %reduce-scatter.35.cloned.1.call-start = ((), (), s32[]{:S(2)}) async-start(), calls=%async_computation.17 | async-start | bytes 589824
  1328.8 187.6 %reduce-scatter.39.cloned.1.call-start = ((), (), s32[]{:S(2)}) async-start(), calls=%async_computation.19 | async-start | bytes 540672
  1380.4 275.6 %all-reduce.25.cloned.1.call-start = ((), (), s32[]{:S(2)}) async-start(), calls=%async_computation.20 | async-start | bytes 6291456
  1391.6 401.9 %reduce-scatter.29.cloned.1.call-start = ((), (), s32[]{:S(2)}) async-start(), calls=%async_computation.14 | async-start | bytes 270336 | tf_op jit(solution)/shard_map/reduce_scatter | solution.py:137
  1401.5 526.2 %reduce-scatter.25.cloned.1.call-start = ((), (), s32[]{:S(2)}) async-start(), calls=%async_computation.12 | async-start | bytes 270336 | tf_op jit(solution)/shard_map/reduce_scatter | solution.py:133
  1430.1 632.1 %reduce-scatter.27.cloned.1.call-start = ((), (), s32[]{:S(2)}) async-start(), calls=%async_computation.13 | async-start | bytes 540672 | tf_op jit(solution)/shard_map/reduce_scatter | solution.py:134
  1434.1 765.5 %reduce-scatter.23.cloned.1.call-start = ((), (), s32[]{:S(2)}) async-start(), calls=%async_computation.11 | async-start | bytes 2162688 | tf_op jit(solution)/shard_map/reduce_scatter | solution.py:131
  (298 other events, 1815.8 us)
Sparse Core Ops, SparseCore 0:
  11.0 56.5 all-gather.7
  70.7 52.7 all-gather.9
  1095.0 14.0 reduce-scatter.36
  1312.3 14.0 reduce-scatter.32
  1328.5 13.1 reduce-scatter.30
  1343.8 13.1 reduce-scatter.34
  1380.5 135.8 reduce-scatter.38
  1521.9 134.0 all-reduce.24
  1658.8 134.6 reduce-scatter.28
  1796.1 131.4 reduce-scatter.24
  1930.5 131.6 reduce-scatter.26
  2064.8 134.6 reduce-scatter.22
where the time goes:
time: 2240 us; the launch traced here: 2210 us
  blocking collectives  758 us (34%)
  waiting for transfers between devices  722 us (32%)
  local copies, waits for them, and re-layouts  478 us (21%)
  matrix products  132 us (6%)
  other arithmetic  71.6 us (3%)
  starting transfers between devices  25.1 us (1%)
    unnamed x728, local copies, waits for them, and re-layouts  182 us
    unnamed x18, waiting for transfers between devices  180 us
    reduce_scatter x1, waiting for transfers between devices, sum_at_end(): lax.psum_scatter(totals[2], ('dp', 'seq'), scatter_dimension=1, tiled=True)  137 us
    reduce_scatter x1, waiting for transfers between devices, sum_at_end(): lax.psum_scatter(totals[8], ('dp', 'seq'), scatter_dimension=1, tiled=True)  135 us
    reduce_scatter x1, waiting for transfers between devices, sum_at_end(): lax.psum_scatter(totals[5], ('dp', 'seq'), scatter_dimension=1, tiled=True)  134 us
    reduce_scatter x1, waiting for transfers between devices, sum_at_end(): lax.psum_scatter(totals[4], ('dp', 'seq'), scatter_dimension=1, tiled=True)  134 us
    rev x4, local copies, waits for them, and re-layouts, relative_shift(): flipped = jnp.flip(scores, -1).reshape(leading + (row_count * span,))  128 us
    unnamed x2, blocking collectives  76.9 us
  transfers between devices with their start and end apart: 20, of which 9 were waited for; matrix products, arithmetic and copies ran while one was open for 21% of the time, Pallas kernels for 0%

commit v1 on v0

--- a/solution.py
+++ b/solution.py
@@ -1,8 +1,11 @@
 import math
+from functools import partial
 
 import jax
 import jax.numpy as jnp
 from jax import lax
+from jax.experimental import pallas as pl
+from jax.experimental.pallas import tpu as pltpu
 from jax.sharding import PartitionSpec as P
 
 HEAD = 64
@@ -536,8 +539,648 @@
         shards[10],
     )
 
+LOW = jnp.bfloat16
+WIDE = jnp.float32
+BLOCK = 256
+AXIS_BITS = (("seq", 1), ("dp", 1), ("dp", 2), ("dp", 4), ("dp", 8))
+ORDER_A = (4, 3, 2, 0, 1)
+ORDER_B = (0, 4, 3, 2, 1)
+ORDER_C = (2, 0, 4, 3, 1)
+EDGE = 16
+CONV_ROWS = 64
+
+
+def swap(value, axis, bit):
+    return lax.ppermute(value, axis, [(i, i ^ bit) for i in range(lax.axis_size(axis))])
+
+
+def gather_chain(block, order):
+    held = block[None]
+    for which in order:
+        held = jnp.concatenate([held, swap(held, *AXIS_BITS[which])], 0)
+    return held
+
+
+def scatter_chain(held, order):
+    for which in reversed(order):
+        half = held.shape[0] // 2
+        arrived = swap(held[half:], *AXIS_BITS[which])
+        total = held[:half].astype(WIDE) + arrived.astype(WIDE)
+        held = total if half == 1 else total.astype(LOW)
+    return held[0]
+
+
+def place(mask, order):
+    return sum(((mask >> which) & 1) << at for at, which in enumerate(order))
+
+
+def nn(a, b):
+    return lax.dot_general(a, b, (((1,), (0,)), ((), ())), preferred_element_type=WIDE)
+
+
+def nt(a, b):
+    return lax.dot_general(a, b, (((1,), (1,)), ((), ())), preferred_element_type=WIDE)
+
+
+def tn(a, b):
+    return lax.dot_general(a, b, (((0,), (0,)), ((), ())), preferred_element_type=WIDE)
+
+
+def normed(value):
+    center = jnp.mean(value, -1, keepdims=True)
+    spread = value - center
+    rate = lax.rsqrt(jnp.mean(spread * spread, -1, keepdims=True) + EPSILON)
+    return spread * rate, rate
+
+
+def normed_back(gradient, unit, rate, gain):
+    inner = gradient * gain
+    mean_one = jnp.mean(inner, -1, keepdims=True)
+    mean_two = jnp.mean(inner * unit, -1, keepdims=True)
+    return (inner - mean_one - unit * mean_two) * rate
+
+
+def column_sum(value):
+    return jnp.sum(value, 0, keepdims=True)
+
+
+def sigmoid(value):
+    return 1.0 / (1.0 + jnp.exp(-value))
+
+
+def rows_at(at, size):
+    return pl.ds(pl.multiple_of(at * size, size), size)
+
+
+def row_numbers(first, size):
+    return first + lax.broadcasted_iota(jnp.int32, (size, 1), 0)
+
+
+def windows(padded, first, size):
+    window = padded[pl.ds(pl.multiple_of(first, size), size + 32), :]
+    for residue in range(8):
+        moved = window[residue : residue + size + 24, :]
+        for step in range(4):
+            offset = 8 * step + residue
+            if offset:
+                yield offset, moved[8 * step : 8 * step + size, :]
+
+
+def gain_row(small, at):
+    return small[at : at + 1, :]
+
+
+def bias_row(small, at):
+    return small[6 + at : 7 + at, :]
+
+
+def tap_row(small, at):
+    return small[20 + at : 21 + at, :]
+
+
+def prep_kernel(meta, ga, gb, wat, wao, wpi, wpo, small, fb, pb, wide, wide_pi, turned):
+    own_a, own_b = meta[2], meta[3]
+    for r in range(32):
+        block = gb[own_b ^ place(r, ORDER_B)].astype(WIDE)
+        rows = slice(8 * r, 8 * r + 8)
+        for k in range(5):
+            wide[k, rows, :] = block[8 * k : 8 * k + 8, :]
+        wide_pi[16 * r : 16 * r + 16, :] = block[40:56, :]
+        wide[5, rows, :] = block[56:64, :]
+        extra = ga[own_a ^ place(r, ORDER_A), 64:80, :].astype(WIDE)
+        turned[rows, :] = extra[0:8, 0:128]
+        pb[0:1, 16 * r : 16 * r + 16] = extra[8:9, 64:80]
+        extra = ga[place(r, ORDER_A), 64:80, :].astype(WIDE)
+        a, c = 32 * place(r, ORDER_A), 32 * place(r, ORDER_C)
+        fb[0:1, a : a + 32] = extra[8:9, 0:32]
+        fb[1:2, c : c + 32] = extra[8:9, 32:64]
+    for k in range(4):
+        wat[k] = wide[k].astype(LOW)
+    wao[...] = wide[4].astype(LOW)
+    wpo[...] = wide[5].astype(LOW)
+    wpi[...] = wide_pi[...].astype(LOW)
+    small[...] = turned[...].T
+
+
+def first_weights(ref):
+    return ref[:, 0:32, :].reshape(-1, ref.shape[2]), ref[:, 32:64, :].reshape(-1, ref.shape[2])
+
+
+def fill_whole(meta, own, other, whole):
+    half = other.shape[0]
+    side = meta[0]
+    whole[pl.ds(pl.multiple_of(side * half, half), half), :] = own[side, 0].astype(WIDE)
+    whole[pl.ds(pl.multiple_of((1 - side) * half, half), half), :] = other[...].astype(WIDE)
+
+
+def rotated(query_position, weight, sine, cosine):
+    lead = nn(query_position, weight)
+    quarter = lead.shape[1] // 2
+    first, second = lead[:, :quarter], lead[:, quarter:]
+    return jnp.concatenate(
+        [second * sine - first * cosine, first * sine + second * cosine], 1
+    ).astype(LOW)
+
+
+def head_scores(qkv, wat, table, table_low, rows, cols):
+    eighth = HEAD ** (-0.5)
+    quarter = table.shape[1] // 2
+    content = (qkv[0, rows, cols].astype(WIDE) * eighth).astype(LOW)
+    position = (qkv[1, rows, cols].astype(WIDE) * eighth).astype(LOW)
+    turned = rotated(
+        position, wat[3, cols, :], table[rows, :quarter], table[rows, quarter:]
+    )
+    return nt(content, qkv[2, :, cols]) + nt(turned, table_low[...])
+
+
+def forward_kernel(
+    meta, own, other, ga, wat, wao, wpi, small, fb, pb, table, table_low,
+    x1, qkv, mixed, logs, x2, gated, filtered, stats, whole, padded,
+):
+    tokens, width = x1.shape
+    length = meta[1]
+    fill_whole(meta, own, other, whole)
+
+    @pl.loop(0, tokens // BLOCK)
+    def _(at):
+        rows = rows_at(at, BLOCK)
+        x = whole[rows, :]
+        low = (normed(x)[0] * gain_row(small, 0) + bias_row(small, 0)).astype(LOW)
+        w_in, w_out = first_weights(ga)
+        hidden = nt(low, w_in) + fb[0:1, :]
+        active = (hidden * sigmoid(hidden)).astype(LOW)
+        value = x + 0.5 * (nn(active, w_out) + bias_row(small, 5))
+        x1[rows, :] = value
+        low = (normed(value)[0] * gain_row(small, 1) + bias_row(small, 1)).astype(LOW)
+        query = nt(low, wat[0]) + bias_row(small, 7)
+        qkv[0, rows, :] = (query + bias_row(small, 10)).astype(LOW)
+        qkv[1, rows, :] = (query + bias_row(small, 11)).astype(LOW)
+        qkv[2, rows, :] = nt(low, wat[1]).astype(LOW)
+        qkv[3, rows, :] = (nt(low, wat[2]) + bias_row(small, 8)).astype(LOW)
+
+    padded[0:EDGE, :] = jnp.zeros((EDGE, width), WIDE)
+    padded[EDGE + tokens : 2 * EDGE + tokens, :] = jnp.zeros((EDGE, width), WIDE)
+
+    @pl.loop(0, tokens // BLOCK)
+    def _(at):
+        rows = rows_at(at, BLOCK)
+        open_keys = lax.broadcasted_iota(jnp.int32, (1, tokens), 1) < length
+        lane = lax.broadcasted_iota(jnp.int32, (1, 128), 1)
+        kept = jnp.zeros((BLOCK, 128), WIDE)
+        for head in range(width // HEAD):
+            cols = slice(head * HEAD, head * HEAD + HEAD)
+            scores = head_scores(qkv, wat, table, table_low, rows, cols)
+            scores = jnp.where(open_keys, scores, MASKED)
+            peak = jnp.max(scores, -1, keepdims=True)
+            raised = jnp.exp(scores - peak)
+            total = jnp.sum(raised, -1, keepdims=True)
+            low = (raised * (1.0 / total)).astype(LOW)
+            mixed[rows, cols] = nn(low, qkv[3, :, cols]).astype(LOW)
+            kept = jnp.where(lane == head, peak + jnp.log(total), kept)
+        logs[rows, :] = kept
+        value = x1[rows, :] + nt(mixed[rows, :], wao[...]) + bias_row(small, 9)
+        x2[rows, :] = value
+        low = (normed(value)[0] * gain_row(small, 2) + bias_row(small, 2)).astype(LOW)
+        joint = nt(low, wpi[...]) + pb[...]
+        valid = (row_numbers(at * BLOCK, BLOCK) < length).astype(WIDE)
+        linear = (joint[:, :width] * sigmoid(joint[:, width:]) * valid).astype(LOW)
+        gated[rows, :] = linear
+        padded[pl.ds(pl.multiple_of(EDGE + at * BLOCK, 16), BLOCK), :] = linear.astype(WIDE)
+
+    @pl.loop(0, tokens // CONV_ROWS)
+    def _(at):
+        total = jnp.zeros((CONV_ROWS, width), WIDE)
+        for offset, piece in windows(padded, at * CONV_ROWS, CONV_ROWS):
+            total = total + piece * tap_row(small, offset - 1)
+        filtered[rows_at(at, CONV_ROWS), :] = total
+
+    count = length.astype(WIDE)
+    valid = (row_numbers(0, tokens) < length).astype(WIDE)
+    total = column_sum(filtered[...] * valid)
+    spread = (filtered[...] - total / count) * valid
+    stats[0:1, :] = total
+    stats[1:2, :] = column_sum(spread * spread)
+    stats[2:3, :] = jnp.zeros((1, width), WIDE) + count
+
+
+def middle_kernel(
+    valid_total,
+    meta, own, other, stats, filtered, x2, wpo, gc, small, fb,
+    keep, send, gx3, shaped_grad, norm_stats, sums, hidden_sum, low_hidden, low_active,
+    low_normed, low_branch, low_swished, low_third, betas, whole, final,
+):
+    tokens, width = x2.shape
+    half = keep.shape[0]
+    side = meta[0]
+    fill_whole(meta, own, other, whole)
+    count = stats[:, 2, :]
+    center = column_sum(stats[:, 0, :]) / valid_total
+    shift = stats[:, 0, :] / count - center
+    variance = column_sum(stats[:, 1, :] + count * shift * shift) / valid_total
+    rate5 = lax.rsqrt(variance + EPSILON)
+    norm_stats[0:1, :] = center
+    norm_stats[1:2, :] = rate5
+    sums[...] = jnp.zeros(sums.shape, WIDE)
+    hidden_sum[...] = jnp.zeros(hidden_sum.shape, WIDE)
+    betas[...] = jnp.zeros(betas.shape, WIDE)
+
+    @pl.loop(0, tokens // BLOCK)
+    def _(at):
+        rows = rows_at(at, BLOCK)
+        standard = (filtered[rows, :] - norm_stats[0:1, :]) * norm_stats[1:2, :]
+        shaped = standard * gain_row(small, 5) + bias_row(small, 13)
+        open5 = sigmoid(shaped)
+        swished = (shaped * open5).astype(LOW)
+        low_swished[rows, :] = swished
+        x3 = x2[rows, :] + nt(swished, wpo[...]) + bias_row(small, 12)
+        unit3, rate3 = normed(x3)
+        low3 = (unit3 * gain_row(small, 3) + bias_row(small, 3)).astype(LOW)
+        low_normed[rows, :] = low3
+        w_in, w_out = first_weights(gc)
+        hidden = nt(low3, w_in) + fb[1:2, :]
+        opened = sigmoid(hidden)
+        active = (hidden * opened).astype(LOW)
+        low_active[rows, :] = active
+        x4 = x3 + 0.5 * (nn(active, w_out) + bias_row(small, 6))
+        unit4, rate4 = normed(x4)
+        final[rows, :] = unit4 * gain_row(small, 4) + bias_row(small, 4)
+        gy = whole[rows, :]
+        sums[0:1, :] += column_sum(gy * unit4)
+        sums[1:2, :] += column_sum(gy)
+        gx4 = normed_back(gy, unit4, rate4, gain_row(small, 4))
+        branch = 0.5 * gx4
+        sums[2:3, :] += column_sum(branch)
+        low_b = branch.astype(LOW)
+        low_branch[rows, :] = low_b
+        hidden_grad = nt(low_b, w_out) * (opened * (1.0 + hidden * (1.0 - opened)))
+        hidden_sum[...] += column_sum(hidden_grad)
+        low_h = hidden_grad.astype(LOW)
+        low_hidden[rows, :] = low_h
+        gn = nn(low_h, w_in)
+        sums[3:4, :] += column_sum(gn * unit3)
+        sums[4:5, :] += column_sum(gn)
+        g3 = gx4 + normed_back(gn, unit3, rate3, gain_row(small, 3))
+        gx3[rows, :] = g3
+        sums[5:6, :] += column_sum(g3)
+        low_g = g3.astype(LOW)
+        low_third[rows, :] = low_g
+        gs = nn(low_g, wpo[...]) * (open5 * (1.0 + shaped * (1.0 - open5)))
+        shaped_grad[rows, :] = gs
+        betas[0:1, :] += column_sum(gs)
+        betas[1:2, :] += column_sum(gs * standard)
+
+    keep[...] = final[pl.ds(pl.multiple_of(side * half, half), half), :].astype(LOW)
+    send[...] = final[pl.ds(pl.multiple_of((1 - side) * half, half), half), :].astype(LOW)
+
+
+def outer_kernel(low_hidden, low_active, low_normed, low_branch, low_swished, low_third, out, wpo_grad):
+    blocks, rows, width = out.shape
+    out[:, 0:32, :] = tn(low_hidden[...], low_normed[...]).astype(LOW).reshape(blocks, 32, width)
+    out[:, 32:64, :] = tn(low_active[...], low_branch[...]).astype(LOW).reshape(blocks, 32, width)
+    wpo_grad[...] = tn(low_third[...], low_swished[...])
+
+
+def back_kernel(
+    valid_total,
+    meta, betas, norm_stats, filtered, shaped_grad, gx3, gated, x2, x1, qkv, mixed, logs,
+    table, table_low, wat, wao, wpi, small, pb, wpo_grad,
+    gx1, out, sums, joint_sum,
+    padded, padded_g, taps, gx2, low_a, mix_grad, query_c, query_p, key_g, value_g, w3_grad, wide, wide_pi,
+):
+    tokens, width = x1.shape
+    length = meta[1]
+    own_b = meta[3]
+    heads = width // HEAD
+    quarter = table.shape[1] // 2
+    eighth = HEAD ** (-0.5)
+    edge = jnp.zeros((EDGE, width), WIDE)
+    for ref in (padded, padded_g):
+        ref[0:EDGE, :] = edge
+        ref[EDGE + tokens : 2 * EDGE + tokens, :] = edge
+    beta = column_sum(betas[:, 0, :]) / valid_total
+    gamma = column_sum(betas[:, 1, :]) / valid_total
+    taps[...] = jnp.zeros(taps.shape, WIDE)
+    sums[...] = jnp.zeros(sums.shape, WIDE)
+    joint_sum[...] = jnp.zeros(joint_sum.shape, WIDE)
+    w3_grad[...] = jnp.zeros(w3_grad.shape, WIDE)
+    key_g[...] = jnp.zeros(key_g.shape, WIDE)
+    value_g[...] = jnp.zeros(value_g.shape, WIDE)
+    wide[1] = jnp.zeros(wide.shape[1:], WIDE)
+    wide_pi[...] = jnp.zeros(wide_pi.shape, WIDE)
+
+    standard = (filtered[...] - norm_stats[0:1, :]) * norm_stats[1:2, :]
+    valid_all = (row_numbers(0, tokens) < length).astype(WIDE)
+    gf = (
+        norm_stats[1:2, :]
+        * gain_row(small, 5)
+        * (shaped_grad[...] - valid_all * (beta + standard * gamma))
+    )
+    padded_g[EDGE : EDGE + tokens, :] = gf.astype(LOW).astype(WIDE)
+    padded[EDGE : EDGE + tokens, :] = gated[...].astype(WIDE)
+
+    @pl.loop(0, tokens // CONV_ROWS)
+    def _(at):
+        here = padded_g[pl.ds(pl.multiple_of(EDGE + at * CONV_ROWS, 16), CONV_ROWS), :]
+        for offset, piece in windows(padded, at * CONV_ROWS, CONV_ROWS):
+            product = (piece * here).reshape(CONV_ROWS // 8, 8, width)
+            taps[offset - 1] += jnp.sum(product, 0)
+        total = jnp.zeros((CONV_ROWS, width), WIDE)
+        for offset, piece in windows(padded_g, at * CONV_ROWS, CONV_ROWS):
+            total = total + piece * tap_row(small, 31 - offset)
+        gx2[rows_at(at, CONV_ROWS), :] = total
+
+    for k in range(31):
+        sums[20 + k : 21 + k, :] = column_sum(taps[k])
+
+    @pl.loop(0, tokens // BLOCK)
+    def _(at):
+        rows = rows_at(at, BLOCK)
+        unit2, rate2 = normed(x2[rows, :])
+        low2 = (unit2 * gain_row(small, 2) + bias_row(small, 2)).astype(LOW)
+        joint = nt(low2, wpi[...]) + pb[...]
+        valid = (row_numbers(at * BLOCK, BLOCK) < length).astype(WIDE)
+        glu = gx2[rows, :] * valid
+        opened = sigmoid(joint[:, width:])
+        joint_grad = jnp.concatenate(
+            [glu * opened, glu * joint[:, :width] * opened * (1.0 - opened)], 1
+        )
+        joint_sum[...] += column_sum(joint_grad)
+        low_j = joint_grad.astype(LOW)
+        wide_pi[...] += tn(low_j, low2)
+        gn = nn(low_j, wpi[...])
+        sums[2:3, :] += column_sum(gn * unit2)
+        sums[8:9, :] += column_sum(gn)
+        g2 = gx3[rows, :] + normed_back(gn, unit2, rate2, gain_row(small, 2))
+        gx2[rows, :] = g2
+        sums[15:16, :] += column_sum(g2)
+        low_g = g2.astype(LOW)
+        low_a[0, rows, :] = low_g
+        mix_grad[rows, :] = nn(low_g, wao[...]).astype(LOW)
+
+    wide[4] = tn(low_a[0], mixed[...])
+
+    @pl.loop(0, tokens // BLOCK)
+    def _(at):
+        rows = rows_at(at, BLOCK)
+        open_keys = lax.broadcasted_iota(jnp.int32, (1, tokens), 1) < length
+        sine, cosine = table[rows, :quarter], table[rows, quarter:]
+        for head in range(heads):
+            cols = slice(head * HEAD, head * HEAD + HEAD)
+            scores = head_scores(qkv, wat, table, table_low, rows, cols)
+            probs = jnp.where(open_keys, jnp.exp(scores - logs[rows, head : head + 1]), 0.0)
+            low_m = mix_grad[rows, cols]
+            value_g[:, cols] += tn(probs.astype(LOW), low_m)
+            pull = nt(low_m, qkv[3, :, cols])
+            delta = jnp.sum(pull * probs, -1, keepdims=True)
+            low_s = (probs * (pull - delta)).astype(LOW)
+            query_c[rows, cols] = nn(low_s, qkv[2, :, cols]) * eighth
+            key_g[:, cols] += tn(low_s, qkv[0, rows, cols]) * eighth
+            turned = nn(low_s, table_low[...]) * eighth
+            one, two = turned[:, :quarter], turned[:, quarter:]
+            lead = jnp.concatenate([two * sine - one * cosine, one * sine + two * cosine], 1)
+            low_l = lead.astype(LOW)
+            query_p[rows, cols] = nt(low_l, wat[3, cols, :])
+            w3_grad[cols, :] += tn(qkv[1, rows, cols], low_l)
+
+    @pl.loop(0, tokens // BLOCK)
+    def _(at):
+        rows = rows_at(at, BLOCK)
+        content, offset = query_c[rows, :], query_p[rows, :]
+        query = content + offset
+        sums[13:14, :] += column_sum(query)
+        sums[14:15, :] += column_sum(value_g[rows, :])
+        sums[16:17, :] += column_sum(content)
+        sums[17:18, :] += column_sum(offset)
+        low_q = query.astype(LOW)
+        low_k = key_g[rows, :].astype(LOW)
+        low_v = value_g[rows, :].astype(LOW)
+        unit1, rate1 = normed(x1[rows, :])
+        low_a[0, rows, :] = low_q
+        low_a[1, rows, :] = low_k
+        low_a[2, rows, :] = low_v
+        low_a[3, rows, :] = (unit1 * gain_row(small, 1) + bias_row(small, 1)).astype(LOW)
+        gn = nn(low_q, wat[0]) + nn(low_k, wat[1]) + nn(low_v, wat[2])
+        sums[1:2, :] += column_sum(gn * unit1)
+        sums[7:8, :] += column_sum(gn)
+        gx1[rows, :] = gx2[rows, :] + normed_back(gn, unit1, rate1, gain_row(small, 1))
+
+    for k in range(3):
+        wide[k] = tn(low_a[k], low_a[3])
+    wide[3] = w3_grad[...]
+    wide[5] = wpo_grad[...]
+    for r in range(32):
+        rows = slice(8 * r, 8 * r + 8)
+        parts = [wide[k, rows, :] for k in range(5)]
+        parts = parts + [wide_pi[16 * r : 16 * r + 16, :], wide[5, rows, :]]
+        out[own_b ^ place(r, ORDER_B)] = jnp.concatenate(parts, 0).astype(LOW)
+
+
+def last_kernel(
+    meta, own, other, ga, gx1, small, fb, sums_mid, hidden_mid, betas, sums_back, joint_sum,
+    keep, send, out,
+    whole, sums, hidden_sum, low_hidden, low_active, low_normed, low_branch, extra, turned,
+):
+    tokens, width = gx1.shape
+    half = keep.shape[0]
+    side = meta[0]
+    own_a = meta[2]
+    fill_whole(meta, own, other, whole)
+    sums[...] = sums_back[...]
+    hidden_sum[...] = jnp.zeros(hidden_sum.shape, WIDE)
+    sums[4:5, :] = sums_mid[0:1, :]
+    sums[10:11, :] = sums_mid[1:2, :]
+    sums[12:13, :] = sums_mid[2:3, :]
+    sums[3:4, :] = sums_mid[3:4, :]
+    sums[9:10, :] = sums_mid[4:5, :]
+    sums[18:19, :] = sums_mid[5:6, :]
+    sums[19:20, :] = betas[0:1, :]
+    sums[5:6, :] = betas[1:2, :]
+
+    @pl.loop(0, tokens // BLOCK)
+    def _(at):
+        rows = rows_at(at, BLOCK)
+        unit0, rate0 = normed(whole[rows, :])
+        low0 = (unit0 * gain_row(small, 0) + bias_row(small, 0)).astype(LOW)
+        low_normed[rows, :] = low0
+        w_in, w_out = first_weights(ga)
+        hidden = nt(low0, w_in) + fb[0:1, :]
+        opened = sigmoid(hidden)
+        low_active[rows, :] = (hidden * opened).astype(LOW)
+        g1 = gx1[rows, :]
+        branch = 0.5 * g1
+        sums[11:12, :] += column_sum(branch)
+        low_b = branch.astype(LOW)
+        low_branch[rows, :] = low_b
+        hidden_grad = nt(low_b, w_out) * (opened * (1.0 + hidden * (1.0 - opened)))
+        hidden_sum[...] += column_sum(hidden_grad)
+        low_h = hidden_grad.astype(LOW)
+        low_hidden[rows, :] = low_h
+        gn = nn(low_h, w_in)
+        sums[0:1, :] += column_sum(gn * unit0)
+        sums[6:7, :] += column_sum(gn)
+        whole[rows, :] = g1 + normed_back(gn, unit0, rate0, gain_row(small, 0))
+
+    keep[...] = whole[pl.ds(pl.multiple_of(side * half, half), half), :]
+    send[...] = whole[pl.ds(pl.multiple_of((1 - side) * half, half), half), :].astype(LOW)
+    blocks = out.shape[0]
+    out[:, 0:32, :] = tn(low_hidden[...], low_normed[...]).astype(LOW).reshape(blocks, 32, width)
+    out[:, 32:64, :] = tn(low_active[...], low_branch[...]).astype(LOW).reshape(blocks, 32, width)
+    extra[...] = jnp.zeros(extra.shape, WIDE)
+    turned[...] = sums[...].T
+    for r in range(32):
+        at = own_a ^ place(r, ORDER_A)
+        extra[at, 0:8, 0:128] = turned[8 * r : 8 * r + 8, :]
+        extra[at, 8:9, 64:80] = joint_sum[0:1, 16 * r : 16 * r + 16]
+        at = place(r, ORDER_A)
+        c = 32 * place(r, ORDER_C)
+        extra[at, 8:9, 0:32] = hidden_sum[0:1, 32 * at : 32 * at + 32]
+        extra[at, 8:9, 32:64] = hidden_mid[0:1, c : c + 32]
+    out[:, 64:80, :] = extra[...].astype(LOW)
+
+
+def call(kernel, outs, scratch, *args):
+    spec = pl.BlockSpec(memory_space=pltpu.VMEM)
+    smem = pl.BlockSpec(memory_space=pltpu.SMEM)
+    return pl.pallas_call(
+        kernel,
+        in_specs=[smem if arg.dtype == jnp.int32 else spec for arg in args],
+        out_specs=[spec] * len(outs),
+        out_shape=[jax.ShapeDtypeStruct(shape, kind) for shape, kind in outs],
+        scratch_shapes=[pltpu.VMEM(shape, kind) for shape, kind in scratch],
+        compiler_params=pltpu.CompilerParams(vmem_limit_bytes=60 * 1024 * 1024),
+    )(*args)
+
+
+def fast_body(
+    inputs, lengths, cotangent, feed_in, feed_in_bias, feed_out, attend_in, attend_out,
+    point_in, point_in_bias, depth_kernel, point_out, gains, biases,
+):
+    micro_count, seq_count, half, width = inputs.shape
+    tokens = half * lax.axis_size("seq")
+    valid_total = float(seq_count * lax.axis_size("dp") * tokens * 3 // 4)
+    side = lax.axis_index("seq")
+    me = lax.axis_index("dp") * 2 + side
+    meta = jnp.stack(
+        [side, lengths[side, 0], place(me, ORDER_A), place(me, ORDER_B)]
+    ).astype(jnp.int32)
+    columns = jnp.concatenate(
+        [feed_in[0], feed_in[1], attend_in[0], attend_in[1], attend_in[2], attend_in[3],
+         attend_out, point_in, point_out], 1,
+    ).T
+    channel = jnp.pad(
+        jnp.concatenate([gains, biases, depth_kernel], 0).T, ((0, 0), (0, width - 51))
+    )
+    extra_row = jnp.pad(
+        jnp.concatenate([feed_in_bias[0], feed_in_bias[1], point_in_bias])[None],
+        ((0, 7), (0, width - 80)),
+    )
+    block_a = jnp.concatenate([columns[0:32], feed_out[0], channel, extra_row], 0)
+    block_b = columns[64:128]
+    block_c = jnp.concatenate([columns[32:64], feed_out[1]], 0)
+    pairs = [(i, 1 - i) for i in range(2)]
+
+    def exchange(value):
+        return lax.ppermute(value, "seq", pairs)
+
+    other = exchange(lax.dynamic_index_in_dim(inputs, 1 - side, 0, False)[0])
+    ga = gather_chain(block_a, ORDER_A)
+    gb = gather_chain(block_b, ORDER_B)
+    gc = gather_chain(block_c, ORDER_C)
+    other_cot = exchange(lax.dynamic_index_in_dim(cotangent, 1 - side, 0, False)[0])
+    table = sinusoid(jnp.arange(tokens, dtype=jnp.int32), width)
+    table_low = table.astype(LOW)
+    square = (width, width)
+    wat, wao, wpi, wpo, small, fb, pb = call(
+        prep_kernel,
+        [((4,) + square, LOW), (square, LOW), ((2 * width, width), LOW), (square, LOW),
+         ((128, width), WIDE), ((2, 1024), WIDE), ((1, 2 * width), WIDE)],
+        [((6,) + square, WIDE), ((2 * width, width), WIDE), ((width, 128), WIDE)],
+        meta, ga, gb,
+    )
+    hidden_width = fb.shape[1]
+    body_shape = (tokens, width)
+    hidden_shape = (tokens, hidden_width)
+    pad_shape = (tokens + 2 * EDGE, width)
+    x1, qkv, mixed, logs, x2, gated, filtered, stats = call(
+        forward_kernel,
+        [(body_shape, WIDE), ((4,) + body_shape, LOW), (body_shape, LOW), ((tokens, 128), WIDE),
+         (body_shape, WIDE), (body_shape, LOW), (body_shape, WIDE), ((3, width), WIDE)],
+        [(body_shape, WIDE), (pad_shape, WIDE)],
+        meta, inputs, other, ga, wat, wao, wpi, small, fb, pb, table, table_low,
+    )
+    dp = lax.axis_size("dp")
+
+    def everywhere(value):
+        spread = jnp.broadcast_to(value[None], (dp,) + value.shape)
+        return lax.all_to_all(spread, "dp", 0, 0, tiled=True)
+
+    all_stats = everywhere(stats)
+    (keep, send, gx3, shaped_grad, norm_stats, sums_mid, hidden_mid, low_hidden, low_active,
+     low_normed, low_branch, low_swished, low_third, betas) = call(
+        partial(middle_kernel, valid_total),
+        [((half, width), LOW), ((half, width), LOW), (body_shape, WIDE), (body_shape, WIDE),
+         ((2, width), WIDE), ((8, width), WIDE), ((1, hidden_width), WIDE), (hidden_shape, LOW),
+         (hidden_shape, LOW), (body_shape, LOW), (body_shape, LOW), (body_shape, LOW),
+         (body_shape, LOW), ((2, width), WIDE)],
+        [(body_shape, WIDE), (body_shape, WIDE)],
+        meta, cotangent, other_cot, all_stats, filtered, x2, wpo, gc, small, fb,
+    )
+    all_betas = everywhere(betas)
+    arrived_out = exchange(send)
+    grads_c, wpo_grad = call(
+        outer_kernel, [(gc.shape, LOW), (square, WIDE)], [],
+        low_hidden, low_active, low_normed, low_branch, low_swished, low_third,
+    )
+    shard_c = scatter_chain(grads_c, ORDER_C)
+    gx1, grads_b, sums_back, joint_sum = call(
+        partial(back_kernel, valid_total),
+        [(body_shape, WIDE), (gb.shape, LOW), ((128, width), WIDE), ((1, 2 * width), WIDE)],
+        [(pad_shape, WIDE), (pad_shape, WIDE), ((31, 8, width), WIDE), (body_shape, WIDE),
+         ((4,) + body_shape, LOW), (body_shape, LOW), (body_shape, WIDE), (body_shape, WIDE),
+         (body_shape, WIDE), (body_shape, WIDE), (square, WIDE), ((6,) + square, WIDE),
+         ((2 * width, width), WIDE)],
+        meta, all_betas, norm_stats, filtered, shaped_grad, gx3, gated, x2, x1, qkv, mixed, logs,
+        table, table_low, wat, wao, wpi, small, pb, wpo_grad,
+    )
+    shard_b = scatter_chain(grads_b, ORDER_B)
+    keep_grad, send_grad, grads_a = call(
+        last_kernel,
+        [((half, width), WIDE), ((half, width), LOW), (ga.shape, LOW)],
+        [(body_shape, WIDE), ((128, width), WIDE), ((1, hidden_width), WIDE), (hidden_shape, LOW),
+         (hidden_shape, LOW), (body_shape, LOW), (body_shape, LOW), ((32, 16, width), WIDE),
+         ((width, 128), WIDE)],
+        meta, inputs, other, ga, gx1, small, fb, sums_mid, hidden_mid, betas, sums_back, joint_sum,
+    )
+    arrived_grad = exchange(send_grad).astype(WIDE)
+    shard_a = scatter_chain(grads_a, ORDER_A)
+
+    def both(mine, theirs):
+        first = jnp.where(side == 0, mine, theirs)
+        second = jnp.where(side == 0, theirs, mine)
+        return jnp.stack([first, second])[:, None]
+
+    turned = jnp.concatenate([shard_a[0:32], shard_c[0:32], shard_b], 0).T
+    channel = shard_a[64:72, 0:51].T
+    row = shard_a[72]
+    return (
+        both(keep, arrived_out),
+        both(keep_grad, arrived_grad),
+        jnp.stack([turned[:, 0:32], turned[:, 32:64]]),
+        jnp.stack([row[0:32], row[32:64]]),
+        jnp.stack([shard_a[32:64], shard_c[32:64]]),
+        jnp.stack([turned[:, 64 + 8 * k : 72 + 8 * k] for k in range(4)]),
+        turned[:, 96:104],
+        turned[:, 104:120],
+        row[64:80],
+        channel[20:51],
+        turned[:, 120:128],
+        channel[0:6],
+        channel[6:20],
+    )
+
 
 def solution(mesh):
+    fast = mesh.shape["seq"] == 2 and mesh.shape["dp"] == 16
     placed = (
         P(None, "dp", "seq", None),
         P(None, "dp"),
@@ -555,7 +1198,7 @@
         P(None, ("dp", "seq")),
     )
     return jax.shard_map(
-        body,
+        fast_body if fast else body,
         mesh=mesh,
         in_specs=placed,
         out_specs=(

time: 2240 us -> 225 us (0.10); the launches traced: 2210 us -> 223 us
  blocking collectives: 758 us -> 0 us
  waiting for transfers between devices: 722 us -> 39.6 us
  local copies, waits for them, and re-layouts: 478 us -> 33.1 us
  matrix products: 132 us -> 0 us
  Pallas kernels: 0 us -> 86.3 us
  other arithmetic: 71.6 us -> 16.1 us
    all_gather x12 -> x0, blocking collectives: 563 us -> none  [the longest x1 71.1 us: fetch_forward(): lax.all_gather(local[8], ('dp', 'seq'), axis=1, tiled=True)]
    reduce_scatter x4 -> x0, waiting for transfers between devices: 541 us -> none  [the longest x1 137 us: sum_at_end(): lax.psum_scatter(totals[2], ('dp', 'seq'), scatter_dimension=1, tiled=True)]
    unnamed x18 -> x0, waiting for transfers between devices: 180 us -> none
    unnamed x728 -> x52, local copies, waits for them, and re-layouts: 182 us -> 16.7 us
    dot_general x81 -> x0, matrix products: 132 us -> none  [the longest x20 27.9 us: outer_sum(): lax.dot_general(left, right, (((0,), (0,)), ((), ())), preferred_element_...]
    rev x4 -> x0, local copies, waits for them, and re-layouts: 128 us -> none  [relative_shift(): flipped = jnp.flip(scores, -1).reshape(leading + (row_count * span,))]
    psum x3 -> x0, blocking collectives: 118 us -> none  [the longest x1 42.4 us: convolution_forward(): lax.psum(jnp.sum(spread * spread, (0, 1)), ('dp', 'seq')) / valid_total]
    reshape x8 -> x0, local copies, waits for them, and re-layouts: 86.4 us -> none  [the longest x2 30.9 us: relative_shift(): return picked.reshape(leading + (row_count, span - 1))[..., :count]]
  transfers between devices with their start and end apart: 20 -> 36, of which waited for: 9 -> 14; matrix products, arithmetic and copies ran while one was open for 21% -> 14% of each run, Pallas kernels for 0% -> 34%
where the time goes in v1:
time: 225 us; the launch traced here: 223 us
  Pallas kernels  86.3 us (38%)
  starting transfers between devices  47.2 us (21%)
  waiting for transfers between devices  39.6 us (18%)
  local copies, waits for them, and re-layouts  33.1 us (15%)
  other arithmetic  16.1 us (7%)
    pallas_call x6, Pallas kernels, call(): pl.pallas_call(kernel, in_specs=[smem if arg.dtype == jnp.int32 else spec...  86.3 us
    ppermute x30, starting transfers between devices, swap(): lax.ppermute(value, axis, [(i, i ^ bit) for i in range(lax.axis_size(axis...  35.5 us
    ppermute x30, waiting for transfers between devices, swap(): lax.ppermute(value, axis, [(i, i ^ bit) for i in range(lax.axis_size(axis...  29.3 us
    unnamed x52, local copies, waits for them, and re-layouts  16.7 us
    all_to_all x2, starting transfers between devices, everywhere(): return lax.all_to_all(spread, 'dp', 0, 0, tiled=True)  7.53 us
    all_to_all x2, waiting for transfers between devices, everywhere(): return lax.all_to_all(spread, 'dp', 0, 0, tiled=True)  6.41 us
  transfers between devices with their start and end apart: 36, of which 14 were waited for; matrix products, arithmetic and copies ran while one was open for 14% of the time, Pallas kernels for 34%

profile of v1, /device:TPU:0, one launch (start us, length us, event | category | flops | bytes accessed | tf_op | source)
XLA Modules:
  0.0 223.4 jit_solution(6024057126569249571)
XLA Ops:
  0.7 0.7 slice_bitcast_fusion.5
  8.3 3.0 %collective-permute-start.12 = (bf16[1,64,256]{2,1,0:T(8,128)(2,1)}, bf16[1,64,256]{2,1,0:T(8,128)(2,1)S(1)}, u32[]{:S(2)}, u32[]{:S(2)}) collective-permute-start(bf16[1,64,256]{2,1,0:T(8,128)(2,1)} %maximum_bitcast_fusion.3), channel_id=1, source_target_pairs={{0,4},{2,6},{4,0},{6,2},{8,12},{10,14},{12,8},{14,10},{16,20},{18,... | collective-permute-start | bytes 98312 | tf_op jit(solution)/shard_map/ppermute | solution.py:554
  11.3 1.5 collective-permute-start.7
  12.8 0.7 slice_bitcast_fusion.16
  13.5 0.8 copy.27
  14.3 0.7 maximum_bitcast_fusion.5
  15.0 0.8 maximum_bitcast_fusion.4
  15.8 2.7 %collective-permute-start.2 = (bf16[1,80,256]{2,1,0:T(8,128)(2,1)S(1)}, bf16[1,80,256]{2,1,0:T(8,128)(2,1)S(1)}, u32[]{:S(2)}, u32[]{:S(2)}) collective-permute-start(bf16[1,80,256]{2,1,0:T(8,128)(2,1)S(1)} %fusion.7), channel_id=1, source_target_pairs={{0,16},{2,18},{4,20},{6,22},{8,24},{10,26},{12,28},{14,30},{16,0},... | collective-permute-start | bytes 122888 | tf_op jit(solution)/shard_map/ppermute | solution.py:554
  18.5 1.6 dynamic-slice_bitcast_fusion
  20.6 1.6 dynamic-slice_bitcast_fusion.1
  22.2 1.5 collective-permute-start
  25.0 1.4 multiply_sine_fusion
  26.4 1.3 constant_dynamic-update-slice_fusion.35
  28.3 0.8 pad_maximum_fusion.9
  31.3 1.6 collective-permute-start.3
  33.6 0.8 pad_maximum_fusion.6
  34.4 2.7 %collective-permute-start.14 = (bf16[4,64,256]{2,1,0:T(8,128)(2,1)S(1)}, bf16[4,64,256]{2,1,0:T(8,128)(2,1)S(1)}, u32[]{:S(2)}, u32[]{:S(2)}) collective-permute-start(bf16[4,64,256]{2,1,0:T(8,128)(2,1)S(1)} %pad_maximum_fusion.6), channel_id=1, source_target_pairs={{0,16},{2,18},{4,20},{6,22},{8,24},{10,26},{12,28},{14,30},{16,0},... | collective-permute-start | bytes 393224 | tf_op jit(solution)/shard_map/ppermute | solution.py:554
  40.1 1.7 collective-permute-done.14
  41.8 0.8 pad_maximum_fusion.3
  42.8 1.4 collective-permute-start.10
  44.2 0.9 collective-permute-done.4
  45.2 1.6 collective-permute-start.5
  46.8 3.1 %collective-permute-done.10 = bf16[8,64,256]{2,1,0:T(8,128)(2,1)S(1)} collective-permute-done((bf16[8,64,256]{2,1,0:T(8,128)(2,1)S(1)}, bf16[8,64,256]{2,1,0:T(8,128)(2,1)S(1)}, u32[]{:S(2)}, u32[]{:S(2)}) %collective-permute-start.10) | collective-permute-done | bytes 262176 | tf_op jit(solution)/shard_map/ppermute | solution.py:554
  50.0 2.3 %collective-permute-done.5 = bf16[8,80,256]{2,1,0:T(8,128)(2,1)S(1)} collective-permute-done((bf16[8,80,256]{2,1,0:T(8,128)(2,1)S(1)}, bf16[8,80,256]{2,1,0:T(8,128)(2,1)S(1)}, u32[]{:S(2)}, u32[]{:S(2)}) %collective-permute-start.5) | collective-permute-done | bytes 327712 | tf_op jit(solution)/shard_map/ppermute | solution.py:554
  53.2 0.9 constant_dynamic-update-slice_fusion.31
  54.6 1.2 pad_add_fusion.meta
  55.8 0.8 fusion.9.table_low
  56.6 0.9 pad_maximum_fusion.table
  57.6 0.9 copy-done.3
  58.5 1.1 copy-done.1
  59.6 2.8 %shard_map.237 = (bf16[4,256,256]{2,1,0:T(8,128)(2,1)}, bf16[256,256]{1,0:T(8,128)(2,1)}, bf16[512,256]{1,0:T(8,128)(2,1)}, bf16[256,256]{1,0:T(8,128)(2,1)}, f3...) custom-call(s32[4]{0:T(128)} %pad_add_fusion.meta, bf16[32,80,256]{2,1,0:T(8,128)(2,1)} %copy-done.1, ...), custom_call_target="tpu_custom_call" | custom-call | tf_op jit(solution)/shard_map/pallas_call | solution.py:1044
  63.1 24.8 %shard_map.238 = (f32[768,256]{1,0:T(8,128)}, bf16[4,768,256]{2,1,0:T(8,128)(2,1)}, bf16[768,256]{1,0:T(8,128)(2,1)}, f32[768,128]{1,0:T(8,128)}, f32[768,256]{1...) custom-call(s32[4]{0:T(128)} %pad_add_fusion.meta, bf16[2,1,384,256]{3,2,1,0:T(8,128)(2,1)} %own.5, ...), custom_call_target="tpu_custom_call" | custom-call | tf_op jit(solution)/shard_map/pallas_call | solution.py:1044
  87.9 1.3 broadcast_in_dim.35
  89.2 3.9 %all-to-all-start = ((f32[16,3,256]{2,1,0:T(4,128)}), f32[16,3,256]{2,1,0:T(4,128)S(1)}, u32[]{:S(2)}, u32[]{:S(2)}) async-start(f32[16,3,256]{2,1,0:T(4,128)} %broadcast_in_dim.35), calls=%async_computation | async-start | bytes 131072 | tf_op jit(solution)/shard_map/all_to_all | solution.py:1115
  93.1 1.1 constant_dynamic-update-slice_fusion.36.gc
  94.2 5.8 %all-to-all-done.stats = f32[16,3,256]{2,1,0:T(4,128)S(1)} async-done(((f32[16,3,256]{2,1,0:T(4,128)}), f32[16,3,256]{2,1,0:T(4,128)S(1)}, u32[]{:S(2)}, u32[]{:S(2)}) %all-to-all-start) | async-done | bytes 49184 | tf_op jit(solution)/shard_map/all_to_all | solution.py:1115
  100.6 10.8 %shard_map.239 = (bf16[384,256]{1,0:T(8,128)(2,1)}, bf16[384,256]{1,0:T(8,128)(2,1)}, f32[768,256]{1,0:T(8,128)}, f32[768,256]{1,0:T(8,128)}, f32[2,256]{1,0:T(2...) custom-call(s32[4]{0:T(128)} %pad_add_fusion.meta, ...), custom_call_target="tpu_custom_call" | custom-call | tf_op jit(solution)/shard_map/pallas_call | solution.py:1044
  111.4 1.9 collective-permute-start.17
  113.3 1.3 broadcast_in_dim.38
  114.6 3.7 %all-to-all-start.1 = ((f32[16,2,256]{2,1,0:T(2,128)}), f32[16,2,256]{2,1,0:T(2,128)S(1)}, u32[]{:S(2)}, u32[]{:S(2)}) async-start(f32[16,2,256]{2,1,0:T(2,128)} %broadcast_in_dim.38), calls=%async_computation.1 | async-start | bytes 65536 | tf_op jit(solution)/shard_map/all_to_all | solution.py:1115
  118.3 4.5 %shard_map.240 = (bf16[32,64,256]{2,1,0:T(8,128)(2,1)}, f32[256,256]{1,0:T(8,128)}) custom-call(bf16[768,1024]{1,0:T(8,128)(2,1)} %get-tuple-element.72.low_hidden, bf16[768,1024]{1,0:T(8,128)(2,1)} %get-tuple-element.73.low_active, bf16[768,256]{1,0:T(8,128)(2,1)} %get-tuple-element.74.low_normed, bf16[768,256]{1,0:T(8,128)(2,1)} %get-tuple-element.75.low_branch, ...), custom_call_target="tpu_custom_call" | custom-call | tf_op jit(solution)/shard_map/pallas_call | solution.py:1044
  122.8 1.1 slice.233
  125.3 35.6 %shard_map.241 = (f32[768,256]{1,0:T(8,128)}, bf16[32,64,256]{2,1,0:T(8,128)(2,1)}, f32[128,256]{1,0:T(8,128)}, f32[1,512]{1,0:T(1,128)}) custom-call(s32[4]{0:T(128)} %pad_add_fusion.meta, f32[16,2,256]{2,1,0:T(2,128)} %copy-done.13, f32[2,256]{1,0:T(2,128)} %get-tuple-element.64.norm_stats, f32[768,256]{1,0:T(8,128)} %get-tuple-element.58.filtered, ...), custom_call_target="tpu_custom_call" | custom-call | tf_op jit(solution)/shard_map/pallas_call | solution.py:1044
  160.9 7.8 %shard_map.242 = (f32[384,256]{1,0:T(8,128)}, bf16[384,256]{1,0:T(8,128)(2,1)}, bf16[32,80,256]{2,1,0:T(8,128)(2,1)}) custom-call(s32[4]{0:T(128)} %pad_add_fusion.meta, bf16[2,1,384,256]{3,2,1,0:T(8,128)(2,1)} %own.5, bf16[384,256]{1,0:T(8,128)(2,1)} %copy-done.8, bf16[32,80,256]{2,1,0:T(8,128)(2,1)} %copy-done.1, f32[768,256]{1,0:T(8,128)} %get-tuple-element.79.gx1, ...), custom_call_target="tpu_custom_call" | custom-call | tf_op jit(solution)/shard_map/pallas_call | solution.py:1044
  169.1 1.2 slice.221
  170.9 0.8 maximum_bitcast_fusion.1
  171.6 3.9 %collective-permute-done.18 = bf16[384,256]{1,0:T(8,128)(2,1)S(1)} collective-permute-done((bf16[384,256]{1,0:T(8,128)(2,1)}, bf16[384,256]{1,0:T(8,128)(2,1)S(1)}, u32[]{:S(2)}, u32[]{:S(2)}) %collective-permute-start.18) | collective-permute-done | bytes 196640 | tf_op jit(solution)/shard_map/ppermute | solution.py:1083
  175.6 0.9 maximum_bitcast_fusion
  177.3 1.7 collective-permute-start.25
  179.2 1.5 collective-permute-start.30
  180.7 4.3 %collective-permute-done.25 = bf16[8,64,256]{2,1,0:T(8,128)(2,1)S(1)} collective-permute-done((bf16[8,64,256]{2,1,0:T(8,128)(2,1)S(1)}, bf16[8,64,256]{2,1,0:T(8,128)(2,1)S(1)}, u32[]{:S(2)}, u32[]{:S(2)}) %collective-permute-start.25) | collective-permute-done | bytes 262176 | tf_op jit(solution)/shard_map/ppermute | solution.py:554
  185.1 2.7 %collective-permute-start.26 = (bf16[4,64,256]{2,1,0:T(8,128)(2,1)S(1)}, bf16[4,64,256]{2,1,0:T(8,128)(2,1)S(1)}, u32[]{:S(2)}, u32[]{:S(2)}) collective-permute-start(bf16[4,64,256]{2,1,0:T(8,128)(2,1)S(1)} %slice.288), channel_id=1, source_target_pairs={{0,16},{2,18},{4,20},{6,22},{8,24},{10,26},{12,28},{14,30},{16,0},... | collective-permute-start | bytes 393224 | tf_op jit(solution)/shard_map/ppermute | solution.py:554
  188.5 4.5 %collective-permute-done.26 = bf16[4,64,256]{2,1,0:T(8,128)(2,1)S(1)} collective-permute-done((bf16[4,64,256]{2,1,0:T(8,128)(2,1)S(1)}, bf16[4,64,256]{2,1,0:T(8,128)(2,1)S(1)}, u32[]{:S(2)}, u32[]{:S(2)}) %collective-permute-start.26) | collective-permute-done | bytes 131104 | tf_op jit(solution)/shard_map/ppermute | solution.py:554
  193.6 0.8 collective-permute-start.31
  194.4 3.1 %collective-permute-done.27 = bf16[2,64,256]{2,1,0:T(8,128)(2,1)S(1)} collective-permute-done((bf16[2,64,256]{2,1,0:T(8,128)(2,1)S(1)}, bf16[2,64,256]{2,1,0:T(8,128)(2,1)S(1)}, u32[]{:S(2)}, u32[]{:S(2)}) %collective-permute-start.27) | collective-permute-done | bytes 65568 | tf_op jit(solution)/shard_map/ppermute | solution.py:554
  197.5 1.6 collective-permute-start.28
  199.2 1.7 collective-permute-start.32
  201.7 1.6 collective-permute-start.21
  203.3 3.8 %collective-permute-done.21 = bf16[4,80,256]{2,1,0:T(8,128)(2,1)S(1)} collective-permute-done((bf16[4,80,256]{2,1,0:T(8,128)(2,1)S(1)}, bf16[4,80,256]{2,1,0:T(8,128)(2,1)S(1)}, u32[]{:S(2)}, u32[]{:S(2)}) %collective-permute-start.21) | collective-permute-done | bytes 163872 | tf_op jit(solution)/shard_map/ppermute | solution.py:554
  207.1 1.7 collective-permute-start.22
  208.8 1.4 collective-permute-start.33
  210.2 1.9 collective-permute-done.22
  212.1 1.8 collective-permute-start.23
  213.9 3.2 %collective-permute-done.23 = bf16[1,80,256]{2,1,0:T(8,128)(2,1)S(1)} collective-permute-done((bf16[1,80,256]{2,1,0:T(8,128)(2,1)S(1)}, bf16[1,80,256]{2,1,0:T(8,128)(2,1)S(1)}, u32[]{:S(2)}, u32[]{:S(2)}) %collective-permute-start.23) | collective-permute-done | bytes 40992 | tf_op jit(solution)/shard_map/ppermute | solution.py:554
  (152 shorter events, 30.3 us)
Async XLA Ops:
  0.6 27.1 %copy-start = (s32[2,1]{0,1:T(1,128)S(1)}, s32[2,1]{0,1:T(1,128)}, u32[]{:S(2)}) copy-start(s32[2,1]{0,1:T(1,128)} %param.15) | copy-start | bytes 28
  7.7 16.7 %copy-start.12 = (bf16[32,256]{1,0:T(8,128)(2,1)}, bf16[32,256]{1,0:T(8,128)(2,1)S(1)}, u32[]{:S(2)}) copy-start(bf16[32,256]{1,0:T(8,128)(2,1)S(1)} %get-tuple-element.138) | copy-start | bytes 49156
  8.3 20.1 %collective-permute-start.12 = (bf16[1,64,256]{2,1,0:T(8,128)(2,1)}, bf16[1,64,256]{2,1,0:T(8,128)(2,1)S(1)}, u32[]{:S(2)}, u32[]{:S(2)}) collective-permute-start(bf16[1,64,256]{2,1,0:T(8,128)(2,1)} %maximum_bitcast_fusion.3), channel_id=1, source_target_pairs={{0,4},{2,6},{4,0},{6,2},{8,12},{10,14},{12,8},{14,10},{16,20},{18,... | collective-permute-start | bytes 98312 | tf_op jit(solution)/shard_map/ppermute | solution.py:554
  11.3 18.4 %collective-permute-start.7 = (bf16[1,64,256]{2,1,0:T(8,128)(2,1)S(1)}, bf16[1,64,256]{2,1,0:T(8,128)(2,1)S(1)}, u32[]{:S(2)}, u32[]{:S(2)}) collective-permute-start(bf16[1,64,256]{2,1,0:T(8,128)(2,1)S(1)} %slice_bitcast_fusion.4), channel_id=1, source_target_pairs={{0,1},{1,0},{2,3},{3,2},{4,5},{5,4},{6,7},{7,6},{8,9},{9,8},{10,11... | collective-permute-start | bytes 98312 | tf_op jit(solution)/shard_map/ppermute | solution.py:554
  15.8 15.5 %collective-permute-start.2 = (bf16[1,80,256]{2,1,0:T(8,128)(2,1)S(1)}, bf16[1,80,256]{2,1,0:T(8,128)(2,1)S(1)}, u32[]{:S(2)}, u32[]{:S(2)}) collective-permute-start(bf16[1,80,256]{2,1,0:T(8,128)(2,1)S(1)} %fusion.7), channel_id=1, source_target_pairs={{0,16},{2,18},{4,20},{6,22},{8,24},{10,26},{12,28},{14,30},{16,0},... | collective-permute-start | bytes 122888 | tf_op jit(solution)/shard_map/ppermute | solution.py:554
  20.1 42.4 %collective-permute-start.1 = (bf16[384,256]{1,0:T(8,128)(2,1)}, bf16[384,256]{1,0:T(8,128)(2,1)S(1)}, u32[]{:S(2)}, u32[]{:S(2)}) collective-permute-start(bf16[384,256]{1,0:T(8,128)(2,1)} %dynamic-slice_bitcast_fusion), channel_id=1, source_target_pairs={{0,1},{1,0},{2,3},{3,2},{4,5},{5,4},{6,7},{7,6},{8,9},{9,8},{10,11... | collective-permute-start | bytes 589832 | tf_op jit(solution)/shard_map/ppermute | solution.py:1083
  22.2 72.0 %collective-permute-start = (bf16[384,256]{1,0:T(8,128)(2,1)}, bf16[384,256]{1,0:T(8,128)(2,1)}, u32[]{:S(2)}, u32[]{:S(2)}) collective-permute-start(bf16[384,256]{1,0:T(8,128)(2,1)} %dynamic-slice_bitcast_fusion.1), channel_id=1, source_target_pairs={{0,1},{1,0},{2,3},{3,2},{4,5},{5,4},{6,7},{7,6},{8,9},{9,8},{10,11... | collective-permute-start | bytes 589832 | tf_op jit(solution)/shard_map/ppermute | solution.py:1083
  29.1 4.5 %collective-permute-start.13 = (bf16[2,64,256]{2,1,0:T(8,128)(2,1)S(1)}, bf16[2,64,256]{2,1,0:T(8,128)(2,1)S(1)}, u32[]{:S(2)}, u32[]{:S(2)}) collective-permute-start(bf16[2,64,256]{2,1,0:T(8,128)(2,1)S(1)} %pad_maximum_fusion.9), channel_id=1, source_target_pairs={{0,1},{1,0},{2,3},{3,2},{4,5},{5,4},{6,7},{7,6},{8,9},{9,8},{10,11... | collective-permute-start | bytes 196616 | tf_op jit(solution)/shard_map/ppermute | solution.py:554
  29.7 7.4 %collective-permute-start.8 = (bf16[2,64,256]{2,1,0:T(8,128)(2,1)S(1)}, bf16[2,64,256]{2,1,0:T(8,128)(2,1)S(1)}, u32[]{:S(2)}, u32[]{:S(2)}) collective-permute-start(bf16[2,64,256]{2,1,0:T(8,128)(2,1)S(1)} %pad_maximum_fusion.8), channel_id=1, source_target_pairs={{0,16},{2,18},{4,20},{6,22},{8,24},{10,26},{12,28},{14,30},{16,0},... | collective-permute-start | bytes 196616 | tf_op jit(solution)/shard_map/ppermute | solution.py:554
  31.3 7.5 %collective-permute-start.3 = (bf16[2,80,256]{2,1,0:T(8,128)(2,1)S(1)}, bf16[2,80,256]{2,1,0:T(8,128)(2,1)S(1)}, u32[]{:S(2)}, u32[]{:S(2)}) collective-permute-start(bf16[2,80,256]{2,1,0:T(8,128)(2,1)S(1)} %pad_maximum_fusion.7), channel_id=1, source_target_pairs={{0,8},{2,10},{4,12},{6,14},{8,0},{10,2},{12,4},{14,6},{16,24},{18,... | collective-permute-start | bytes 245768 | tf_op jit(solution)/shard_map/ppermute | solution.py:554
  34.4 7.4 %collective-permute-start.14 = (bf16[4,64,256]{2,1,0:T(8,128)(2,1)S(1)}, bf16[4,64,256]{2,1,0:T(8,128)(2,1)S(1)}, u32[]{:S(2)}, u32[]{:S(2)}) collective-permute-start(bf16[4,64,256]{2,1,0:T(8,128)(2,1)S(1)} %pad_maximum_fusion.6), channel_id=1, source_target_pairs={{0,16},{2,18},{4,20},{6,22},{8,24},{10,26},{12,28},{14,30},{16,0},... | collective-permute-start | bytes 393224 | tf_op jit(solution)/shard_map/ppermute | solution.py:554
  37.0 5.7 %collective-permute-start.9 = (bf16[4,64,256]{2,1,0:T(8,128)(2,1)S(1)}, bf16[4,64,256]{2,1,0:T(8,128)(2,1)S(1)}, u32[]{:S(2)}, u32[]{:S(2)}) collective-permute-start(bf16[4,64,256]{2,1,0:T(8,128)(2,1)S(1)} %pad_maximum_fusion.5), channel_id=1, source_target_pairs={{0,8},{2,10},{4,12},{6,14},{8,0},{10,2},{12,4},{14,6},{16,24},{18,... | collective-permute-start | bytes 393224 | tf_op jit(solution)/shard_map/ppermute | solution.py:554
  38.2 8.6 %copy-start.15 = (bf16[16,64,256]{2,1,0:T(8,128)(2,1)S(1)}, bf16[16,64,256]{2,1,0:T(8,128)(2,1)}, u32[]{:S(2)}) copy-start(bf16[16,64,256]{2,1,0:T(8,128)(2,1)} %get-tuple-element.140) | copy-start | bytes 1572868
  38.9 6.3 %collective-permute-start.4 = (bf16[4,80,256]{2,1,0:T(8,128)(2,1)S(1)}, bf16[4,80,256]{2,1,0:T(8,128)(2,1)S(1)}, u32[]{:S(2)}, u32[]{:S(2)}) collective-permute-start(bf16[4,80,256]{2,1,0:T(8,128)(2,1)S(1)} %pad_maximum_fusion.4), channel_id=1, source_target_pairs={{0,4},{2,6},{4,0},{6,2},{8,12},{10,14},{12,8},{14,10},{16,20},{18,... | collective-permute-start | bytes 491528 | tf_op jit(solution)/shard_map/ppermute | solution.py:554
  40.1 6.7 %copy-start.14 = (bf16[16,80,256]{2,1,0:T(8,128)(2,1)S(1)}, bf16[16,80,256]{2,1,0:T(8,128)(2,1)}, u32[]{:S(2)}) copy-start(bf16[16,80,256]{2,1,0:T(8,128)(2,1)} %get-tuple-element.132) | copy-start | bytes 1966084
  42.6 10.6 %collective-permute-start.15 = (bf16[8,64,256]{2,1,0:T(8,128)(2,1)S(1)}, bf16[8,64,256]{2,1,0:T(8,128)(2,1)S(1)}, u32[]{:S(2)}, u32[]{:S(2)}) collective-permute-start(bf16[8,64,256]{2,1,0:T(8,128)(2,1)S(1)} %pad_maximum_fusion.3), channel_id=1, source_target_pairs={{0,8},{2,10},{4,12},{6,14},{8,0},{10,2},{12,4},{14,6},{16,24},{18,... | collective-permute-start | bytes 786440 | tf_op jit(solution)/shard_map/ppermute | solution.py:554
  42.8 7.1 %collective-permute-start.10 = (bf16[8,64,256]{2,1,0:T(8,128)(2,1)S(1)}, bf16[8,64,256]{2,1,0:T(8,128)(2,1)S(1)}, u32[]{:S(2)}, u32[]{:S(2)}) collective-permute-start(bf16[8,64,256]{2,1,0:T(8,128)(2,1)S(1)} %pad_maximum_fusion.2), channel_id=1, source_target_pairs={{0,4},{2,6},{4,0},{6,2},{8,12},{10,14},{12,8},{14,10},{16,20},{18,... | collective-permute-start | bytes 786440 | tf_op jit(solution)/shard_map/ppermute | solution.py:554
  45.2 7.1 %collective-permute-start.5 = (bf16[8,80,256]{2,1,0:T(8,128)(2,1)S(1)}, bf16[8,80,256]{2,1,0:T(8,128)(2,1)S(1)}, u32[]{:S(2)}, u32[]{:S(2)}) collective-permute-start(bf16[8,80,256]{2,1,0:T(8,128)(2,1)S(1)} %pad_maximum_fusion.1), channel_id=1, source_target_pairs={{0,1},{1,0},{2,3},{3,2},{4,5},{5,4},{6,7},{7,6},{8,9},{9,8},{10,11... | collective-permute-start | bytes 983048 | tf_op jit(solution)/shard_map/ppermute | solution.py:554
  49.9 7.6 %collective-permute-start.11 = (bf16[16,64,256]{2,1,0:T(8,128)(2,1)S(1)}, bf16[16,64,256]{2,1,0:T(8,128)(2,1)S(1)}, u32[]{:S(2)}, u32[]{:S(2)}) collective-permute-start(bf16[16,64,256]{2,1,0:T(8,128)(2,1)S(1)} %get-tuple-element.110), channel_id=1, source_target_pairs={{0,2},{2,0},{4,6},{6,4},{8,10},{10,8},{12,14},{14,12},{16,18},{18,... | collective-permute-start | bytes 1572872 | tf_op jit(solution)/shard_map/ppermute | solution.py:554
  52.4 5.2 %collective-permute-start.6 = (bf16[16,80,256]{2,1,0:T(8,128)(2,1)S(1)}, bf16[16,80,256]{2,1,0:T(8,128)(2,1)S(1)}, u32[]{:S(2)}, u32[]{:S(2)}) collective-permute-start(bf16[16,80,256]{2,1,0:T(8,128)(2,1)S(1)} %get-tuple-element.106), channel_id=1, source_target_pairs={{0,2},{2,0},{4,6},{6,4},{8,10},{10,8},{12,14},{14,12},{16,18},{18,... | collective-permute-start | bytes 1966088 | tf_op jit(solution)/shard_map/ppermute | solution.py:554
  54.1 39.0 %collective-permute-start.16 = (bf16[16,64,256]{2,1,0:T(8,128)(2,1)}, bf16[16,64,256]{2,1,0:T(8,128)(2,1)}, u32[]{:S(2)}, u32[]{:S(2)}) collective-permute-start(bf16[16,64,256]{2,1,0:T(8,128)(2,1)} %get-tuple-element.108), channel_id=1, source_target_pairs={{0,2},{2,0},{4,6},{6,4},{8,10},{10,8},{12,14},{14,12},{16,18},{18,... | collective-permute-start | bytes 1572872 | tf_op jit(solution)/shard_map/ppermute | solution.py:554
  57.6 1.0 copy-start.3
  58.5 1.1 copy-start.1
  62.4 0.7 copy-start.8
  63.1 30.0 %copy-start.4 = (bf16[32,64,256]{2,1,0:T(8,128)(2,1)S(1)}, bf16[32,64,256]{2,1,0:T(8,128)(2,1)}, u32[]{:S(2)}) copy-start(bf16[32,64,256]{2,1,0:T(8,128)(2,1)} %get-tuple-element.109) | copy-start | bytes 3145732
  89.2 10.8 %all-to-all-start = ((f32[16,3,256]{2,1,0:T(4,128)}), f32[16,3,256]{2,1,0:T(4,128)S(1)}, u32[]{:S(2)}, u32[]{:S(2)}) async-start(f32[16,3,256]{2,1,0:T(4,128)} %broadcast_in_dim.35), calls=%async_computation | async-start | bytes 131072 | tf_op jit(solution)/shard_map/all_to_all | solution.py:1115
  94.2 5.8 %copy-start.5 = (bf16[32,64,256]{2,1,0:T(8,128)(2,1)}, bf16[32,64,256]{2,1,0:T(8,128)(2,1)S(1)}, u32[]{:S(2)}) copy-start(bf16[32,64,256]{2,1,0:T(8,128)(2,1)S(1)} %constant_dynamic-update-slice_fusion.36.gc) | copy-start | bytes 3145732
  100.0 0.6 copy-start.10
  111.4 59.4 %collective-permute-start.17 = (bf16[384,256]{1,0:T(8,128)(2,1)}, bf16[384,256]{1,0:T(8,128)(2,1)S(1)}, u32[]{:S(2)}, u32[]{:S(2)}) collective-permute-start(bf16[384,256]{1,0:T(8,128)(2,1)} %get-tuple-element.62), channel_id=1, source_target_pairs={{0,1},{1,0},{2,3},{3,2},{4,5},{5,4},{6,7},{7,6},{8,9},{9,8},{10,11... | collective-permute-start | bytes 589832 | tf_op jit(solution)/shard_map/ppermute | solution.py:1083
  114.6 10.1 %all-to-all-start.1 = ((f32[16,2,256]{2,1,0:T(2,128)}), f32[16,2,256]{2,1,0:T(2,128)S(1)}, u32[]{:S(2)}, u32[]{:S(2)}) async-start(f32[16,2,256]{2,1,0:T(2,128)} %broadcast_in_dim.38), calls=%async_computation.1 | async-start | bytes 65536 | tf_op jit(solution)/shard_map/all_to_all | solution.py:1115
  123.9 52.7 %collective-permute-start.24 = (bf16[16,64,256]{2,1,0:T(8,128)(2,1)S(1)}, bf16[16,64,256]{2,1,0:T(8,128)(2,1)S(1)}, u32[]{:S(2)}, u32[]{:S(2)}) collective-permute-start(bf16[16,64,256]{2,1,0:T(8,128)(2,1)S(1)} %slice.233), channel_id=1, source_target_pairs={{0,2},{2,0},{4,6},{6,4},{8,10},{10,8},{12,14},{14,12},{16,18},{18,... | collective-permute-start | bytes 1572872 | tf_op jit(solution)/shard_map/ppermute | solution.py:554
  124.7 0.6 copy-start.13
  160.9 8.0 %copy-start.7 = (bf16[32,64,256]{2,1,0:T(8,128)(2,1)S(1)}, bf16[32,64,256]{2,1,0:T(8,128)(2,1)}, u32[]{:S(2)}) copy-start(bf16[32,64,256]{2,1,0:T(8,128)(2,1)} %get-tuple-element.88) | copy-start | bytes 3145732
  168.8 2.1 copy-start.11
  168.8 6.8 %collective-permute-start.18 = (bf16[384,256]{1,0:T(8,128)(2,1)}, bf16[384,256]{1,0:T(8,128)(2,1)S(1)}, u32[]{:S(2)}, u32[]{:S(2)}) collective-permute-start(bf16[384,256]{1,0:T(8,128)(2,1)} %get-tuple-element.85), channel_id=1, source_target_pairs={{0,1},{1,0},{2,3},{3,2},{4,5},{5,4},{6,7},{7,6},{8,9},{9,8},{10,11... | collective-permute-start | bytes 589832 | tf_op jit(solution)/shard_map/ppermute | solution.py:1083
  169.0 10.0 %collective-permute-start.29 = (bf16[16,64,256]{2,1,0:T(8,128)(2,1)S(1)}, bf16[16,64,256]{2,1,0:T(8,128)(2,1)S(1)}, u32[]{:S(2)}, u32[]{:S(2)}) collective-permute-start(bf16[16,64,256]{2,1,0:T(8,128)(2,1)S(1)} %slice.245), channel_id=1, source_target_pairs={{0,2},{2,0},{4,6},{6,4},{8,10},{10,8},{12,14},{14,12},{16,18},{18,... | collective-permute-start | bytes 1572872 | tf_op jit(solution)/shard_map/ppermute | solution.py:554
  169.1 6.5 %copy-start.9 = (f32[384,256]{1,0:T(8,128)S(1)}, f32[384,256]{1,0:T(8,128)}, u32[]{:S(2)}) copy-start(f32[384,256]{1,0:T(8,128)} %get-tuple-element.84) | copy-start | bytes 1179652
  170.3 17.5 %collective-permute-start.19 = (bf16[16,80,256]{2,1,0:T(8,128)(2,1)S(1)}, bf16[16,80,256]{2,1,0:T(8,128)(2,1)S(1)}, u32[]{:S(2)}, u32[]{:S(2)}) collective-permute-start(bf16[16,80,256]{2,1,0:T(8,128)(2,1)S(1)} %slice.221), channel_id=1, source_target_pairs={{0,2},{2,0},{4,6},{6,4},{8,10},{10,8},{12,14},{14,12},{16,18},{18,... | collective-permute-start | bytes 1966088 | tf_op jit(solution)/shard_map/ppermute | solution.py:554
  175.6 1.5 copy-start.6
  177.3 10.5 %copy-start.2 = (bf16[32,80,256]{2,1,0:T(8,128)(2,1)S(1)}, bf16[32,80,256]{2,1,0:T(8,128)(2,1)}, u32[]{:S(2)}) copy-start(bf16[32,80,256]{2,1,0:T(8,128)(2,1)} %get-tuple-element.86) | copy-start | bytes 3932164
  177.3 7.7 %collective-permute-start.25 = (bf16[8,64,256]{2,1,0:T(8,128)(2,1)S(1)}, bf16[8,64,256]{2,1,0:T(8,128)(2,1)S(1)}, u32[]{:S(2)}, u32[]{:S(2)}) collective-permute-start(bf16[8,64,256]{2,1,0:T(8,128)(2,1)S(1)} %slice.286), channel_id=1, source_target_pairs={{0,8},{2,10},{4,12},{6,14},{8,0},{10,2},{12,4},{14,6},{16,24},{18,... | collective-permute-start | bytes 786440 | tf_op jit(solution)/shard_map/ppermute | solution.py:554
  179.2 14.4 %collective-permute-start.30 = (bf16[8,64,256]{2,1,0:T(8,128)(2,1)S(1)}, bf16[8,64,256]{2,1,0:T(8,128)(2,1)S(1)}, u32[]{:S(2)}, u32[]{:S(2)}) collective-permute-start(bf16[8,64,256]{2,1,0:T(8,128)(2,1)S(1)} %slice.295), channel_id=1, source_target_pairs={{0,4},{2,6},{4,0},{6,2},{8,12},{10,14},{12,8},{14,10},{16,20},{18,... | collective-permute-start | bytes 786440 | tf_op jit(solution)/shard_map/ppermute | solution.py:554
  185.1 7.9 %collective-permute-start.26 = (bf16[4,64,256]{2,1,0:T(8,128)(2,1)S(1)}, bf16[4,64,256]{2,1,0:T(8,128)(2,1)S(1)}, u32[]{:S(2)}, u32[]{:S(2)}) collective-permute-start(bf16[4,64,256]{2,1,0:T(8,128)(2,1)S(1)} %slice.288), channel_id=1, source_target_pairs={{0,16},{2,18},{4,20},{6,22},{8,24},{10,26},{12,28},{14,30},{16,0},... | collective-permute-start | bytes 393224 | tf_op jit(solution)/shard_map/ppermute | solution.py:554
  188.0 13.5 %collective-permute-start.20 = (bf16[8,80,256]{2,1,0:T(8,128)(2,1)S(1)}, bf16[8,80,256]{2,1,0:T(8,128)(2,1)S(1)}, u32[]{:S(2)}, u32[]{:S(2)}) collective-permute-start(bf16[8,80,256]{2,1,0:T(8,128)(2,1)S(1)} %slice.277), channel_id=1, source_target_pairs={{0,1},{1,0},{2,3},{3,2},{4,5},{5,4},{6,7},{7,6},{8,9},{9,8},{10,11... | collective-permute-start | bytes 983048 | tf_op jit(solution)/shard_map/ppermute | solution.py:554
  193.0 4.5 %collective-permute-start.27 = (bf16[2,64,256]{2,1,0:T(8,128)(2,1)S(1)}, bf16[2,64,256]{2,1,0:T(8,128)(2,1)S(1)}, u32[]{:S(2)}, u32[]{:S(2)}) collective-permute-start(bf16[2,64,256]{2,1,0:T(8,128)(2,1)S(1)} %slice.290), channel_id=1, source_target_pairs={{0,1},{1,0},{2,3},{3,2},{4,5},{5,4},{6,7},{7,6},{8,9},{9,8},{10,11... | collective-permute-start | bytes 196616 | tf_op jit(solution)/shard_map/ppermute | solution.py:554
  193.6 5.5 %collective-permute-start.31 = (bf16[4,64,256]{2,1,0:T(8,128)(2,1)S(1)}, bf16[4,64,256]{2,1,0:T(8,128)(2,1)S(1)}, u32[]{:S(2)}, u32[]{:S(2)}) collective-permute-start(bf16[4,64,256]{2,1,0:T(8,128)(2,1)S(1)} %slice.297), channel_id=1, source_target_pairs={{0,8},{2,10},{4,12},{6,14},{8,0},{10,2},{12,4},{14,6},{16,24},{18,... | collective-permute-start | bytes 393224 | tf_op jit(solution)/shard_map/ppermute | solution.py:554
  197.5 4.0 %collective-permute-start.28 = (bf16[1,64,256]{2,1,0:T(8,128)(2,1)S(1)}, bf16[1,64,256]{2,1,0:T(8,128)(2,1)S(1)}, u32[]{:S(2)}, u32[]{:S(2)}) collective-permute-start(bf16[1,64,256]{2,1,0:T(8,128)(2,1)S(1)} %slice.292), channel_id=1, source_target_pairs={{0,4},{2,6},{4,0},{6,2},{8,12},{10,14},{12,8},{14,10},{16,20},{18,... | collective-permute-start | bytes 98312 | tf_op jit(solution)/shard_map/ppermute | solution.py:554
  199.2 9.6 %collective-permute-start.32 = (bf16[2,64,256]{2,1,0:T(8,128)(2,1)S(1)}, bf16[2,64,256]{2,1,0:T(8,128)(2,1)S(1)}, u32[]{:S(2)}, u32[]{:S(2)}) collective-permute-start(bf16[2,64,256]{2,1,0:T(8,128)(2,1)S(1)} %slice.299), channel_id=1, source_target_pairs={{0,16},{2,18},{4,20},{6,22},{8,24},{10,26},{12,28},{14,30},{16,0},... | collective-permute-start | bytes 196616 | tf_op jit(solution)/shard_map/ppermute | solution.py:554
  201.7 5.4 %collective-permute-start.21 = (bf16[4,80,256]{2,1,0:T(8,128)(2,1)S(1)}, bf16[4,80,256]{2,1,0:T(8,128)(2,1)S(1)}, u32[]{:S(2)}, u32[]{:S(2)}) collective-permute-start(bf16[4,80,256]{2,1,0:T(8,128)(2,1)S(1)} %slice.279), channel_id=1, source_target_pairs={{0,4},{2,6},{4,0},{6,2},{8,12},{10,14},{12,8},{14,10},{16,20},{18,... | collective-permute-start | bytes 491528 | tf_op jit(solution)/shard_map/ppermute | solution.py:554
  207.1 4.9 %collective-permute-start.22 = (bf16[2,80,256]{2,1,0:T(8,128)(2,1)S(1)}, bf16[2,80,256]{2,1,0:T(8,128)(2,1)S(1)}, u32[]{:S(2)}, u32[]{:S(2)}) collective-permute-start(bf16[2,80,256]{2,1,0:T(8,128)(2,1)S(1)} %slice.281), channel_id=1, source_target_pairs={{0,8},{2,10},{4,12},{6,14},{8,0},{10,2},{12,4},{14,6},{16,24},{18,... | collective-permute-start | bytes 245768 | tf_op jit(solution)/shard_map/ppermute | solution.py:554
  208.8 5.1 %collective-permute-start.33 = (bf16[1,64,256]{2,1,0:T(8,128)(2,1)S(1)}, bf16[1,64,256]{2,1,0:T(8,128)(2,1)S(1)}, u32[]{:S(2)}, u32[]{:S(2)}) collective-permute-start(bf16[1,64,256]{2,1,0:T(8,128)(2,1)S(1)} %slice.301), channel_id=1, source_target_pairs={{0,1},{1,0},{2,3},{3,2},{4,5},{5,4},{6,7},{7,6},{8,9},{9,8},{10,11... | collective-permute-start | bytes 98312 | tf_op jit(solution)/shard_map/ppermute | solution.py:554
  212.1 5.0 %collective-permute-start.23 = (bf16[1,80,256]{2,1,0:T(8,128)(2,1)S(1)}, bf16[1,80,256]{2,1,0:T(8,128)(2,1)S(1)}, u32[]{:S(2)}, u32[]{:S(2)}) collective-permute-start(bf16[1,80,256]{2,1,0:T(8,128)(2,1)S(1)} %slice.283), channel_id=1, source_target_pairs={{0,16},{2,18},{4,20},{6,22},{8,24},{10,26},{12,28},{14,30},{16,0},... | collective-permute-start | bytes 122888 | tf_op jit(solution)/shard_map/ppermute | solution.py:554
